TPU v7x, 512 devices: a whole 4x8x8 slice. The times are simulated.
512 devices in a mesh: lon: 32 (over z_hi, y, core), lat: 16 (over z_lo, x).
Axes of the slice: x: 4, y: 8, z: 8 (z_hi: 2, z_lo: 4; z = z_hi * 4 + z_lo), core: 2. Of those that a mesh axis runs over, the one named last changes fastest.
Arguments:
- tracer: float32 [8, 2048, 8192], P(None, 'lat', 'lon'), may hold values from -8 to 8
- courant: float32 [8, 2048, 8192], P(None, 'lat', 'lon'), may hold values from 0.25 to 40960
- hop_counts: int32 [2048], P('lat'), may hold values from 0 to 7, as said below
- row_area: float32 [2048], P('lat'), may hold values from 1 to 10
Outputs:
- updated: float32 [8, 2048, 8192], P(None, 'lat', 'lon')
- dateline_flux: float32 [8], replicated
Inputs may be any that keep to these rules, and one draw needn't show every extreme that they name: `hop_counts`: only the first 8 and the last 8 latitude rows may have counts above 0.
All inputs are finite; a program needn't handle non-finite values.
Results may differ from a plain program's by a relative error of at most 0.0003.
Values sent between devices are 32-bit elements; how exact they have to be, the bound alone decides.
No kernel may reach another device: no remote copies, remote signals or barrier semaphores. Data moves between devices by JAX's collectives and lax.ppermute only.
A program may use at most 64 MiB of HBM per device.

v0:
```python
import jax
import jax.numpy as jnp
from jax import lax
from jax.sharding import PartitionSpec as P

STOPS = 7


def from_behind(array, axis, by):
    devices = lax.axis_size(axis)
    return lax.ppermute(array, axis, [(i, (i + by) % devices) for i in range(devices)])


def prefix(part, axis, combine, identity):
    place = lax.axis_index(axis)
    gathered = jax.tree.map(lambda a: lax.all_gather(a, axis), part)
    state = jax.tree.map(lambda a, e: jnp.zeros_like(a) + jnp.asarray(e, a.dtype), part, identity)

    def one(hop, state):
        return combine(
            state, jax.tree.map(lambda a: lax.dynamic_index_in_dim(a, hop, 0, False), gathered)
        )

    return lax.fori_loop(0, place, one, state)


def broadcast(block, axis, source):
    block = jnp.where(lax.axis_index(axis) == source, block, jnp.zeros_like(block))
    return lax.psum(block, axis)


def compose(earlier, latter):
    return (earlier[0] * latter[0], latter[0] * earlier[1] + latter[1])


def hop_slabs(slab_rows, counts):
    for bit_index in range(STOPS.bit_length()):
        arrived = from_behind(slab_rows, "lon", 1 << bit_index)
        chosen = jnp.right_shift(counts, bit_index) % 2 == 1
        slab_rows = jnp.where(chosen[None, :, None], arrived, slab_rows)
    return slab_rows


def within_block(factors, source):
    growth = factors
    offset = factors * source
    length = factors.shape[-1]
    stride = 1
    while stride < length:
        lead_growth = jnp.concatenate(
            [jnp.ones_like(growth[..., :stride]), growth[..., :-stride]], axis=-1
        )
        lead_offset = jnp.concatenate(
            [jnp.zeros_like(offset[..., :stride]), offset[..., :-stride]], axis=-1
        )
        offset = growth * lead_offset + offset
        growth = growth * lead_growth
        stride = stride * 2
    return (growth, offset)


def body(tracer, courant, hop_counts, row_area):
    source = hop_slabs(tracer, hop_counts)
    factors = courant / (1.0 + courant)
    growth, offset = within_block(factors, source)
    own_map = (growth[..., -1], offset[..., -1])
    identity = (jnp.ones_like(own_map[0]), jnp.zeros_like(own_map[1]))
    prior_growth, prior_offset = prefix(own_map, "lon", compose, identity)
    whole_map = compose((prior_growth, prior_offset), own_map)
    stacked = broadcast(jnp.stack(whole_map), "lon", lax.axis_size("lon") - 1)
    loop_growth = stacked[0]
    loop_offset = stacked[1]
    wrap = loop_offset / (1.0 - loop_growth)
    inflow = prior_growth * wrap + prior_offset
    flux = growth * inflow[..., None] + offset
    before = jnp.concatenate([inflow[..., None], flux[..., :-1]], axis=-1)
    updated = (source + before) / (1.0 + courant)
    weighted = jnp.sum(row_area[None, :] * wrap, axis=1)
    weighted_sum, area_sum = lax.psum((weighted, jnp.sum(row_area)), "lat")
    return (updated, weighted_sum / area_sum)


def solution(mesh):
    return jax.shard_map(
        body,
        mesh=mesh,
        in_specs=(P(None, "lat", "lon"), P(None, "lat", "lon"), P("lat"), P("lat")),
        out_specs=(P(None, "lat", "lon"), P()),
        check_vma=False,
    )
```

profile of v0, /device:TPU:256, one launch (start us, length us, event | category | flops | bytes accessed | tf_op | source)
XLA Modules:
  0.0 374.7 jit_solution(12177327457562862417)
XLA Ops:
  0.6 1.7 copy.24
  2.3 1.9 collective-permute-start
  4.3 31.8 %collective-permute-done = f32[8,128,256]{1,0,2:T(8,128)S(1)} collective-permute-done((f32[8,128,256]{1,0,2:T(8,128)S(1)}, f32[8,128,256]{1,0,2:T(8,128)S(1)}, u32[]{:S(2)}, u32[]{:S(2)}) %collective-permute-start) | collective-permute-done | bytes 1048608 | tf_op jit(solution)/shard_map/ppermute | solution.py:11
  36.2 1.9 collective-permute-start.1
  38.1 45.9 %collective-permute-done.1 = f32[8,128,256]{1,0,2:T(8,128)S(1)} collective-permute-done((f32[8,128,256]{1,0,2:T(8,128)S(1)}, f32[8,128,256]{1,0,2:T(8,128)S(1)}, u32[]{:S(2)}, u32[]{:S(2)}) %collective-permute-start.1) | collective-permute-done | bytes 1048608 | tf_op jit(solution)/shard_map/ppermute | solution.py:11
  84.1 1.9 collective-permute-start.2
  86.1 1.6 copy.27
  87.7 0.6 copy-done.3
  88.4 0.6 reduce_sum.19
  89.0 47.8 %collective-permute-done.2 = f32[8,128,256]{1,0,2:T(8,128)S(1)} collective-permute-done((f32[8,128,256]{1,0,2:T(8,128)S(1)}, f32[8,128,256]{1,0,2:T(8,128)S(1)}, u32[]{:S(2)}, u32[]{:S(2)}) %collective-permute-start.2) | collective-permute-done | bytes 1048608 | tf_op jit(solution)/shard_map/ppermute | solution.py:11
  137.0 0.8 copy-done.1
  137.9 0.3 multiply_add_fusion.7
  138.3 0.3 multiply_add_fusion.6
  138.7 0.3 multiply_add_fusion.5
  140.9 46.4 %all-gather = f32[256,128,1]{1,0,2:T(8,128)S(1)} all-gather(f32[8,128,1]{1,0,2:T(8,128)S(1)} %slice.92), channel_id=2, replica_groups=mesh['lon'=32,'lat'=16] {'lon'}, dimensions={0}, use_global_device_ids=true | all-gather | bytes 135168 | tf_op jit(solution)/shard_map/all_gather | solution.py:16
  187.3 48.3 %all-gather.1 = f32[256,128,1]{1,0,2:T(8,128)S(1)} all-gather(f32[8,128,1]{1,0,2:T(8,128)S(1)} %slice.101), channel_id=3, replica_groups=mesh['lon'=32,'lat'=16] {'lon'}, dimensions={0}, use_global_device_ids=true | all-gather | bytes 135168 | tf_op jit(solution)/shard_map/all_gather | solution.py:16
  235.6 0.6 while.12
  236.2 0.7 fusion.4
  236.9 85.6 %psum.21 = f32[2,8,128]{2,1,0:T(8,128)S(1)} all-reduce(f32[2,8,128]{2,1,0:T(8,128)S(1)} %maximum_select_fusion), channel_id=1, replica_groups=mesh['lon'=32,'lat'=16] {'lon'}, use_global_device_ids=true, to_apply=%region_2.3 | all-reduce | flops 2048 | bytes 16384 | tf_op jit(solution)/shard_map/psum | solution.py:29
  322.7 1.4 slice_add_fusion
  324.2 0.3 add_divide_fusion
  324.5 1.4 copy.28
  325.9 47.7 %all-reduce.16 = (f32[8]{0:T(128)S(1)}, f32[]{:T(128)}) all-reduce(f32[8]{0:T(128)S(1)} %get-tuple-element.74, f32[]{:T(128)} %reduce_sum.19), channel_id=1, replica_groups=mesh['lon'=32,'lat'=16] {'lat'}, use_global_device_ids=true, to_apply=%region_4.5 | all-reduce | flops 9 | bytes 72 | tf_op jit(solution)/shard_map/psum | solution.py:79
  373.5 1.1 broadcast_divide_fusion
  (56 shorter events, 2.9 us)
Async XLA Ops:
  0.6 3.6 copy-start.4
  2.3 33.7 %collective-permute-start = (f32[8,128,256]{1,0,2:T(8,128)S(1)}, f32[8,128,256]{1,0,2:T(8,128)S(1)}, u32[]{:S(2)}, u32[]{:S(2)}) collective-permute-start(f32[8,128,256]{1,0,2:T(8,128)S(1)} %copy.24), channel_id=1, source_target_pairs={{0,16},{16,32},{32,48},{48,64},{64,80},{80,96},{96,112},{112,128},... | collective-permute-start | bytes 3145736 | tf_op jit(solution)/shard_map/ppermute | solution.py:11
  36.2 47.9 %collective-permute-start.1 = (f32[8,128,256]{1,0,2:T(8,128)S(1)}, f32[8,128,256]{1,0,2:T(8,128)S(1)}, u32[]{:S(2)}, u32[]{:S(2)}) collective-permute-start(f32[8,128,256]{1,0,2:T(8,128)S(1)} %broadcast_select_fusion), channel_id=1, source_target_pairs={{0,32},{16,48},{32,64},{48,80},{64,96},{80,112},{96,128},{112,144}... | collective-permute-start | bytes 3145736 | tf_op jit(solution)/shard_map/ppermute | solution.py:11
  84.1 52.7 %collective-permute-start.2 = (f32[8,128,256]{1,0,2:T(8,128)S(1)}, f32[8,128,256]{1,0,2:T(8,128)S(1)}, u32[]{:S(2)}, u32[]{:S(2)}) collective-permute-start(f32[8,128,256]{1,0,2:T(8,128)S(1)} %broadcast_select_fusion.1), channel_id=1, source_target_pairs={{0,64},{16,80},{32,96},{48,112},{64,128},{80,144},{96,160},{112,17... | collective-permute-start | bytes 3145736 | tf_op jit(solution)/shard_map/ppermute | solution.py:11
  87.7 0.7 copy-start.3
  136.8 1.0 copy-start.1
  140.7 46.5 %copy-start = (f32[8,128,256]{1,0,2:T(8,128)}, f32[8,128,256]{1,0,2:T(8,128)S(1)}, u32[]{:S(2)}) copy-start(f32[8,128,256]{1,0,2:T(8,128)S(1)} %get-tuple-element.54) | copy-start | bytes 3145732
  322.7 1.5 copy-start.2
where the time goes:
time: 375 us
  blocking collectives  228 us (61%)
  waiting for transfers between devices  126 us (34%)
  local copies, waits for them, and re-layouts  7.22 us (2%)
  other arithmetic  6.81 us (2%)
  starting transfers between devices  5.76 us (2%)
    ppermute x3, waiting for transfers between devices, from_behind(): lax.ppermute(array, axis, [(i, (i + by) % devices) for i in range(devices)])  126 us
    all_gather x2, blocking collectives, prefix(): gathered = jax.tree.map(lambda a: lax.all_gather(a, axis), part)  94.7 us
    psum x1, blocking collectives, broadcast(): return lax.psum(block, axis)  85.6 us
    psum x1, blocking collectives, body(): weighted_sum, area_sum = lax.psum((weighted, jnp.sum(row_area)), 'lat')  47.7 us
  transfers between devices with their start and end apart: 3, of which 3 were waited for; matrix products, arithmetic and copies ran while one was open for 1% of the time, Pallas kernels for 0%

commit v1 on v0

v1 whole, which is shorter than its diff:
```python
import jax
import jax.numpy as jnp
from jax import lax
from jax.experimental import pallas as pl
from jax.experimental.pallas import tpu as pltpu
from jax.sharding import Mesh, PartitionSpec as P

HALVES, RING, LEVELS, ROWS, CELLS, SLAB = 2, 16, 8, 128, 256, 8
SEGMENTS = 8
STEPS = CELLS // SEGMENTS
SENT = 40
BACK = 16

VMEM = pl.BlockSpec(memory_space=pltpu.VMEM)
SMEM = pl.BlockSpec(memory_space=pltpu.SMEM)


def lanes(shape):
    return lax.broadcasted_iota(jnp.int32, shape, len(shape) - 1)


def scan_segments(source, courant, put):
    growth = jnp.ones((SEGMENTS, ROWS), jnp.float32)
    offset = jnp.zeros((SEGMENTS, ROWS), jnp.float32)
    for step in range(STEPS):
        at = pl.ds(step, SEGMENTS, stride=STEPS)
        c = courant[at, :]
        inverse = 1.0 / (1.0 + c)
        factor = c * inverse
        total = source[at, :] + offset
        put(at, total * inverse, growth * inverse)
        offset = factor * total
        growth = growth * factor
    place = lax.broadcasted_iota(jnp.int32, (SEGMENTS, ROWS), 0)
    for stride in (1, 2, 4):
        inside = place >= stride
        offset = jnp.where(inside, growth * pltpu.roll(offset, stride, 0) + offset, offset)
        growth = jnp.where(inside, growth * pltpu.roll(growth, stride, 0), growth)
    entry_growth = jnp.where(place >= 1, pltpu.roll(growth, 1, 0), 1.0)
    entry_offset = jnp.where(place >= 1, pltpu.roll(offset, 1, 0), 0.0)
    return entry_growth, entry_offset, growth[-1:], offset[-1:]


def maps_kernel(tracer, courant, maps, part, slope, entry, source_t, courant_t, ends):
    def level(l, slot):
        source_t[slot] = tracer[l].T
        courant_t[slot] = courant[l].T

        def put(at, a, b):
            part[l, at, :] = a
            slope[l, at, :] = b

        g, o, end_g, end_o = scan_segments(source_t.at[slot], courant_t.at[slot], put)
        entry[l, 0] = g
        entry[l, 1] = o
        ends[0, pl.ds(l, 1), :] = end_g
        ends[1, pl.ds(l, 1), :] = end_o

    def pair(i, carry):
        level(2 * i, 0)
        level(2 * i + 1, 1)
        return carry

    lax.fori_loop(0, LEVELS // 2, pair, 0)
    low = lanes((LEVELS, ROWS)) < 64
    g, o = ends[0], ends[1]
    maps[0] = jnp.where(low, g, pltpu.roll(o, 64, 1))
    maps[1] = jnp.where(low, pltpu.roll(g, 64, 1), o)


def local_maps(tracer, courant):
    f32 = jnp.float32
    shape = jax.ShapeDtypeStruct
    return pl.pallas_call(
        maps_kernel,
        out_shape=(
            shape((2, LEVELS, ROWS), f32),
            shape((LEVELS, CELLS, ROWS), f32),
            shape((LEVELS, CELLS, ROWS), f32),
            shape((LEVELS, 2, SEGMENTS, ROWS), f32),
        ),
        in_specs=[VMEM, VMEM],
        out_specs=(VMEM, VMEM, VMEM, VMEM),
        scratch_shapes=[
            pltpu.VMEM((2, CELLS, ROWS), f32),
            pltpu.VMEM((2, CELLS, ROWS), f32),
            pltpu.VMEM((2, LEVELS, ROWS), f32),
        ],
        name="local_maps",
    )(tracer, courant)


def turn_kernel(part, slope, entry, part_out, slope_out, buffer):
    def level(l, slot):
        g, o = entry[l, 0], entry[l, 1]
        for step in range(STEPS):
            at = pl.ds(step, SEGMENTS, stride=STEPS)
            b = slope[l, at, :]
            buffer[slot, 0, at, :] = part[l, at, :] + b * o
            buffer[slot, 1, at, :] = b * g
        part_out[l] = buffer[slot, 0].T
        slope_out[l] = buffer[slot, 1].T

    def pair(i, carry):
        level(2 * i, 0)
        level(2 * i + 1, 1)
        return carry

    lax.fori_loop(0, LEVELS // 2, pair, 0)


def turn(part, slope, entry):
    shape = jax.ShapeDtypeStruct((LEVELS, ROWS, CELLS), jnp.float32)
    return pl.pallas_call(
        turn_kernel,
        out_shape=(shape, shape),
        in_specs=[VMEM, VMEM, VMEM],
        out_specs=(VMEM, VMEM),
        scratch_shapes=[pltpu.VMEM((2, 2, CELLS, ROWS), jnp.float32)],
        name="turn",
    )(part, slope, entry)


def pack_kernel(own, partner, own_maps, partner_maps, sent):
    for r in range(SLAB):
        for a in range(4):
            ref = own if a < 2 else partner
            for half in range(2):
                x = ref[2 * (a % 2) + half, pl.ds(r, LEVELS, stride=SLAB), :]
                to = pl.ds(8 * a + 4 * half, 4)
                sent[2 * r, to, :] = x[:4]
                sent[2 * r + 1, to, :] = x[4:]
    zeros = jnp.zeros((SENT - 32, 128), jnp.float32)
    for l in range(LEVELS):
        for parity in range(2):
            sent[2 * l + parity, pl.ds(32, SENT - 32), :] = zeros
            sent[2 * l + parity, pl.ds(32, 1), :] = own_maps[parity, pl.ds(l, 1), :]
            sent[2 * l + parity, pl.ds(33, 1), :] = partner_maps[parity, pl.ds(l, 1), :]


def pack(own, partner, own_maps, partner_maps):
    return pl.pallas_call(
        pack_kernel,
        out_shape=jax.ShapeDtypeStruct((RING, SENT, 128), jnp.float32),
        in_specs=[VMEM] * 4,
        out_specs=VMEM,
        name="pack",
    )(own, partner, own_maps, partner_maps)


def solve_kernel(scalars, weights, got, back, source, courant, source_t, courant_t, part, slope):
    hop, half, level, parity = scalars[0], scalars[1], scalars[2], scalars[3]
    for d in range(HALVES * RING):
        base = (d % RING) * SENT + (0 if d < RING else 16)
        for side in range(2):
            to = pl.ds(side * 128, 128)
            source[pl.ds(4 * d, 4), to] = got[pl.ds(base + 4 * side, 4), :]
            courant[pl.ds(4 * d, 4), to] = got[pl.ds(base + 8 + 4 * side, 4), :]
    source_t[...] = pltpu.roll(source[...].T, 4 * hop, 1)
    courant_t[...] = courant[...].T

    def put(at, a, b):
        part[at, :] = a
        slope[at, :] = b

    entry_g, entry_o, g, o = scan_segments(source_t, courant_t, put)
    for stride in (4, 8, 16, 32, 64):
        o = g * pltpu.roll(o, stride, 1) + o
        g = g * pltpu.roll(g, stride, 1)
    inflow = pltpu.roll(o / (1.0 - g), 4, 1)
    entry = entry_g * inflow + entry_o
    for step in range(STEPS):
        at = pl.ds(step, SEGMENTS, stride=STEPS)
        source_t[at, :] = part[at, :] + slope[at, :] * entry
    source[...] = source_t[...].T
    x = jnp.concatenate([got[pl.ds(32, RING, stride=SENT), :], got[pl.ds(33, RING, stride=SENT), :]], 0)
    low = lanes(x.shape) < 64
    turned = pltpu.roll(x, 64, 1)
    rest_g = jnp.where(low, x, turned)
    rest_o = jnp.where(low, turned, x)
    for stride in (1, 2, 4, 8, 16):
        rest_o = rest_g * pltpu.roll(rest_o, stride, 0) + rest_o
        rest_g = rest_g * pltpu.roll(rest_g, stride, 0)
    rest = pltpu.roll(rest_o / (1.0 - rest_g), 1, 0)
    wrap = jnp.where(half == 0, rest[:1], rest[RING : RING + 1])
    own = jnp.sum(wrap * weights[pl.ds(0, 1), :], axis=1, keepdims=True)
    lane = lanes((1, 128))
    slab = pltpu.roll(inflow, (4 * parity + 128 - 64 * half) % 128, 1) * weights[pl.ds(1, 1), :]
    means = jnp.where(lane == level, own, 0.0) + jnp.where((lane >= 4 * parity) & (lane < 4 * parity + 4), slab, 0.0)
    zeros = jnp.zeros((BACK - 8, 128), jnp.float32)
    for d in range(RING):
        for side in range(2):
            back[d, pl.ds(4 * side, 4), :] = source[pl.ds(4 * d, 4), pl.ds(side * 128, 128)]
        back[d, pl.ds(8, BACK - 8), :] = zeros
        back[d, pl.ds(8, 1), :] = rest[d : d + 1]
        back[d, pl.ds(9, 1), :] = means


def solve(scalars, weights, got):
    f32 = jnp.float32
    return pl.pallas_call(
        solve_kernel,
        out_shape=jax.ShapeDtypeStruct((RING, BACK, 128), f32),
        in_specs=[SMEM, VMEM, VMEM],
        out_specs=VMEM,
        scratch_shapes=[pltpu.VMEM((ROWS, CELLS), f32)] * 2 + [pltpu.VMEM((CELLS, ROWS), f32)] * 4,
        name="solve",
    )(scalars, weights, got)


def finish_kernel(scalars, part, slope, got, updated):
    low = lanes((LEVELS, ROWS)) < 64
    even = got[pl.ds(8, LEVELS, stride=2 * BACK), :]
    odd = got[pl.ds(8 + BACK, LEVELS, stride=2 * BACK), :]
    inflow = jnp.where(low, even, pltpu.roll(odd, 64, 1))
    columns = jnp.concatenate([inflow] * 16, axis=0).T
    for l in range(LEVELS):
        updated[l] = part[l] + slope[l] * columns[:, l : l + 1]

    @pl.when(scalars[0] == 1)
    def _():
        rows = pl.ds(pl.multiple_of(scalars[1], SLAB), SLAB)
        for l in range(LEVELS):
            for side in range(2):
                at = (l // 4) * BACK + 4 * side + l % 4
                updated[l, rows, pl.ds(side * 128, 128)] = got[pl.ds(at, SLAB, stride=2 * BACK), :]


def finish(scalars, part, slope, got):
    return pl.pallas_call(
        finish_kernel,
        out_shape=jax.ShapeDtypeStruct((LEVELS, ROWS, CELLS), jnp.float32),
        in_specs=[SMEM, VMEM, VMEM, VMEM],
        out_specs=VMEM,
        name="finish",
    )(scalars, part, slope, got)


def body(tracer, courant, hop_counts, row_area):
    lat = lax.axis_index("lat")
    lats = lax.axis_size("lat")
    half = lax.axis_index("half")
    ring = lax.axis_index("ring")
    last = lat == lats - 1
    polar = (lat == 0) | last
    start = jnp.where(last, ROWS - SLAB, 0)

    def slab_of(a):
        a = lax.dynamic_slice_in_dim(a, start, SLAB, 1).reshape(LEVELS * SLAB, CELLS)
        return a[:, :128], a[:, 128:]

    own = jnp.stack([*slab_of(tracer), *slab_of(courant)])

    def across(i):
        h, rest = divmod(i, RING * lats)
        moved = rest % lats in (0, lats - 1)
        return (i, (1 - h) * RING * lats + rest if moved else i)

    every = ("half", "ring", "lat")
    partner = lax.ppermute(own, every, [across(i) for i in range(HALVES * RING * lats)])
    maps, part, slope, entry = local_maps(tracer, courant)
    partner_maps = lax.ppermute(maps, "half", [(0, 1), (1, 0)])
    part, slope = turn(part, slope, entry)

    sent = pack(own, partner, maps, partner_maps)
    got = lax.all_to_all(sent, "ring", 0, 0, tiled=True)

    row = ring // 2
    parity = ring % 2
    position = jnp.arange(ROWS)
    in_slab = polar & (position >= start) & (position < start + SLAB)
    others = jnp.where(in_slab, 0.0, row_area)
    others = jnp.where(parity == 0, others, jnp.roll(others, -64))
    others = jnp.where(position < 64, others, 0.0)
    slab_area = jnp.where(polar, lax.dynamic_index_in_dim(row_area, start + row, 0, False), 0.0)
    weights = jnp.stack([others, jnp.broadcast_to(slab_area, (ROWS,))])
    hop = lax.dynamic_index_in_dim(hop_counts, start + row, 0, False)
    scalars = jnp.stack([hop, half, row, parity]).astype(jnp.int32)
    back = solve(scalars, weights, got.reshape(RING * SENT, 128))
    back = lax.all_to_all(back, "ring", 0, 0, tiled=True)

    sums = jnp.sum(back[:, 9, :], axis=0)
    sums = jnp.where(position == LEVELS, jnp.sum(row_area), sums)
    sums = lax.all_to_all(jnp.broadcast_to(sums, (lats, 1, ROWS)), "lat", 0, 0, tiled=True)
    sums = jnp.sum(sums, axis=(0, 1))
    updated = finish(
        jnp.stack([polar, start]).astype(jnp.int32), part, slope, back.reshape(RING * BACK, 128)
    )
    return updated, sums[:LEVELS] / sums[LEVELS]


def solution(mesh):
    split = Mesh(mesh.devices.reshape(HALVES, RING, -1), ("half", "ring", "lat"))
    field = P(None, "lat", ("half", "ring"))
    return jax.shard_map(
        body,
        mesh=split,
        in_specs=(field, field, P("lat"), P("lat")),
        out_specs=(field, P()),
        check_vma=False,
    )
```

time: 375 us -> 87.7 us (0.23)
  the two profiles are of different devices: /device:TPU:256 before, /device:TPU:1 now
where the time goes in v1:
time: 87.7 us; the launch traced here: 87.1 us
  starting transfers between devices  32.7 us (37%)
  waiting for transfers between devices  23.4 us (27%)
  Pallas kernels  19.3 us (22%)
  local copies, waits for them, and re-layouts  6.08 us (7%)
  other arithmetic  4.26 us (5%)
  between operations  1.37 us (2%)
    ppermute x1, starting transfers between devices, body(): lax.ppermute(own, every, [across(i) for i in range(HALVES * RING * lats)])  11.5 us
    all_to_all x1, starting transfers between devices, body(): got = lax.all_to_all(sent, 'ring', 0, 0, tiled=True)  9.35 us
    all_to_all x1, waiting for transfers between devices, body(): back = lax.all_to_all(back, 'ring', 0, 0, tiled=True)  8.46 us
    all_to_all x1, waiting for transfers between devices, body(): got = lax.all_to_all(sent, 'ring', 0, 0, tiled=True)  8.39 us
    all_to_all x1, starting transfers between devices, body(): lax.all_to_all(jnp.broadcast_to(sums, (lats, 1, ROWS)), 'lat', 0, 0, tile...  6.59 us
    ppermute x1, waiting for transfers between devices, body(): partner_maps = lax.ppermute(maps, 'half', [(0, 1), (1, 0)])  6.57 us
    pallas_call x1, Pallas kernels, local_maps(): pl.pallas_call(maps_kernel, out_shape=(shape((2, LEVELS, ROWS), f32), sha...  6.01 us
    pallas_call x1, Pallas kernels, turn(): pl.pallas_call(turn_kernel, out_shape=(shape, shape), in_specs=[VMEM, VME...  5.66 us
  transfers between devices with their start and end apart: 5, of which 3 were waited for; matrix products, arithmetic and copies ran while one was open for 5% of the time, Pallas kernels for 17%

profile of v1, /device:TPU:1, one launch (start us, length us, event | category | flops | bytes accessed | tf_op | source)
XLA Modules:
  0.0 87.1 jit_solution(1984915496836149371)
XLA Ops:
  0.6 0.9 %dynamic-slice_bitcast_fusion = (f32[64,256]{1,0:T(8,128)S(1)}, f32[64,256]{1,0:T(8,128)S(1)}) fusion(f32[8,128,256]{2,1,0:T(8,128)} %courant.1, s32[]{:T(128)} %select_n.47, f32[8,128,256]{2,1,0:T(8,128)} %tracer.1), kind=kLoop, calls=%fused_computation.1 | loop fusion | bytes 262148 | tf_op jit(solution)/shard_map/reshape | solution.py:249
  1.6 11.5 %collective-permute-start = (f32[4,64,128]{2,1,0:T(8,128)S(1)}, f32[4,64,128]{2,1,0:T(8,128)S(1)}, u32[]{:S(2)}, u32[]{:S(2)}) collective-permute-start(f32[4,64,128]{2,1,0:T(8,128)S(1)} %pad_maximum_fusion.own), channel_id=1, source_target_pairs={{0,256},{1,1},{2,2},{3,3},{4,4},{5,5},{6,6},{7,7},{8,8},{9,9},{10,... | collective-permute-start | bytes 393224 | tf_op jit(solution)/shard_map/ppermute | solution.py:260
  13.0 6.0 %local_maps.1 = (f32[2,8,128]{2,1,0:T(8,128)}, f32[8,256,128]{2,1,0:T(8,128)}, f32[8,256,128]{2,1,0:T(8,128)}, f32[8,2,8,128]{3,2,1,0:T(8,128)}) custom-call(f32[8,128,256]{2,1,0:T(8,128)} %tracer.1, f32[8,128,256]{2,1,0:T(8,128)} %courant.1), custom_call_target="tpu_custom_call" | custom-call | tf_op jit(solution)/shard_map/local_maps/pallas_call | solution.py:74
  19.1 1.9 %collective-permute-start.1 = (f32[2,8,128]{2,1,0:T(8,128)}, f32[2,8,128]{2,1,0:T(8,128)S(1)}, u32[]{:S(2)}, u32[]{:S(2)}) collective-permute-start(f32[2,8,128]{2,1,0:T(8,128)} %get-tuple-element.13.own_maps), channel_id=1, source_target_pairs={{0,256},{256,0},{1,257},{257,1},{2,258},{258,2},{3,259},{259,3},{4... | collective-permute-start | bytes 24584 | tf_op jit(solution)/shard_map/ppermute | solution.py:262
  21.0 6.6 %collective-permute-done.1.partner_maps = f32[2,8,128]{2,1,0:T(8,128)S(1)} collective-permute-done((f32[2,8,128]{2,1,0:T(8,128)}, f32[2,8,128]{2,1,0:T(8,128)S(1)}, u32[]{:S(2)}, u32[]{:S(2)}) %collective-permute-start.1) | collective-permute-done | bytes 8224 | tf_op jit(solution)/shard_map/ppermute | solution.py:262
  27.6 0.6 copy-done.4
  28.2 0.7 copy-done.3
  28.8 1.8 %pack.1 = f32[16,40,128]{2,1,0:T(8,128)} custom-call(f32[4,64,128]{2,1,0:T(8,128)} %copy-done.2, f32[4,64,128]{2,1,0:T(8,128)} %copy-done.3, f32[2,8,128]{2,1,0:T(8,128)} %get-tuple-element.13.own_maps, f32[2,8,128]{2,1,0:T(8,128)} %copy-done.4), custom_call_target="tpu_custom_call" | custom-call | tf_op jit(solution)/shard_map/pack/pallas_call | solution.py:142
  30.6 9.3 %all-to-all-start = ((f32[16,40,128]{2,1,0:T(8,128)}), f32[16,40,128]{2,1,0:T(8,128)S(1)}, u32[]{:S(2)}, u32[]{:S(2)}) async-start(f32[16,40,128]{2,1,0:T(8,128)} %pack.1), calls=%async_computation | async-start | bytes 655360 | tf_op jit(solution)/shard_map/all_to_all | solution.py:266
  40.5 0.6 dynamic_slice.15
  41.2 0.7 dynamic_slice.14
  42.6 0.6 stack.55.weights
  43.2 1.3 %pad_add_fusion.1.scalars = s32[4]{0:T(128)} fusion(s32[1]{0:T(128)} %bitcast.4, s32[1]{0:T(128)} %bitcast.3, s32[1]{0:T(128)} %bitcast.2, s32[1]{0:T(128)} %dynamic_slice.14), kind=kLoop, calls=%fused_computation.13 | loop fusion | flops 12 | bytes 32 | tf_op jit(solution)/shard_map/stack | solution.py:278
  44.5 8.4 %all-to-all-done = f32[16,40,128]{2,1,0:T(8,128)S(1)} async-done(((f32[16,40,128]{2,1,0:T(8,128)}), f32[16,40,128]{2,1,0:T(8,128)S(1)}, u32[]{:S(2)}, u32[]{:S(2)}) %all-to-all-start) | async-done | bytes 327712 | tf_op jit(solution)/shard_map/all_to_all | solution.py:266
  52.9 0.7 copy-done
  53.7 2.9 %solve.1 = f32[16,16,128]{2,1,0:T(8,128)} custom-call(s32[4]{0:T(128)} %pad_add_fusion.1.scalars, f32[2,128]{1,0:T(2,128)} %stack.55.weights, f32[640,128]{1,0:T(8,128)} %bitcast.24), custom_call_target="tpu_custom_call" | custom-call | tf_op jit(solution)/shard_map/solve/pallas_call | solution.py:201
  56.5 3.4 %all-to-all-start.1 = ((f32[16,16,128]{2,1,0:T(8,128)}), f32[16,16,128]{2,1,0:T(8,128)S(1)}, u32[]{:S(2)}, u32[]{:S(2)}) async-start(f32[16,16,128]{2,1,0:T(8,128)} %solve.1), calls=%async_computation.1 | async-start | bytes 262144 | tf_op jit(solution)/shard_map/all_to_all | solution.py:280
  59.9 8.5 %all-to-all-done.1 = f32[16,16,128]{2,1,0:T(8,128)S(1)} async-done(((f32[16,16,128]{2,1,0:T(8,128)}), f32[16,16,128]{2,1,0:T(8,128)S(1)}, u32[]{:S(2)}, u32[]{:S(2)}) %all-to-all-start.1) | async-done | bytes 131104 | tf_op jit(solution)/shard_map/all_to_all | solution.py:280
  69.0 0.6 broadcast_in_dim.15
  69.6 6.6 %all-to-all-start.2 = ((f32[16,1,128]{2,1,0:T(1,128)}), f32[16,1,128]{2,1,0:T(1,128)S(1)}, u32[]{:S(2)}, u32[]{:S(2)}) async-start(f32[16,1,128]{2,1,0:T(1,128)} %broadcast_in_dim.15), calls=%async_computation.2 | async-start | bytes 16384 | tf_op jit(solution)/shard_map/all_to_all | solution.py:284
  76.2 0.6 pad_add_fusion.scalars
  76.8 5.7 %turn.1 = (f32[8,128,256]{2,1,0:T(8,128)}, f32[8,128,256]{2,1,0:T(8,128)}) custom-call(f32[8,256,128]{2,1,0:T(8,128)} %get-tuple-element.8.part, f32[8,256,128]{2,1,0:T(8,128)} %get-tuple-element.9.slope, f32[8,2,8,128]{3,2,1,0:T(8,128)} %get-tuple-element.10.entry), custom_call_target="tpu_custom_call" | custom-call | tf_op jit(solution)/shard_map/turn/pallas_call | solution.py:114
  82.5 3.0 %finish.1 = f32[8,128,256]{2,1,0:T(8,128)} custom-call(s32[2]{0:T(128)} %pad_add_fusion.scalars, f32[8,128,256]{2,1,0:T(8,128)} %get-tuple-element.11.part, f32[8,128,256]{2,1,0:T(8,128)} %get-tuple-element.12.slope, f32[256,128]{1,0:T(8,128)} %bitcast.25), custom_call_target="tpu_custom_call" | custom-call | tf_op jit(solution)/shard_map/finish/pallas_call | solution.py:230
  86.1 1.1 %slice_divide_fusion = f32[8]{0:T(128)} fusion(f32[128]{0:T(128)S(1)} %reduce_sum.29, f32[]{:T(128)} %bitcast.16), kind=kLoop, calls=%fused_computation.14 | loop fusion | flops 8 | bytes 68 | tf_op jit(solution)/shard_map/div | solution.py:289
  (23 shorter events, 2.0 us)
Async XLA Ops:
  1.6 17.5 %copy-start.2 = (f32[4,64,128]{2,1,0:T(8,128)}, f32[4,64,128]{2,1,0:T(8,128)S(1)}, u32[]{:S(2)}) copy-start(f32[4,64,128]{2,1,0:T(8,128)S(1)} %pad_maximum_fusion.own) | copy-start | bytes 393220
  1.6 26.0 %collective-permute-start = (f32[4,64,128]{2,1,0:T(8,128)S(1)}, f32[4,64,128]{2,1,0:T(8,128)S(1)}, u32[]{:S(2)}, u32[]{:S(2)}) collective-permute-start(f32[4,64,128]{2,1,0:T(8,128)S(1)} %pad_maximum_fusion.own), channel_id=1, source_target_pairs={{0,256},{1,1},{2,2},{3,3},{4,4},{5,5},{6,6},{7,7},{8,8},{9,9},{10,... | collective-permute-start | bytes 393224 | tf_op jit(solution)/shard_map/ppermute | solution.py:260
  19.1 8.5 %collective-permute-start.1 = (f32[2,8,128]{2,1,0:T(8,128)}, f32[2,8,128]{2,1,0:T(8,128)S(1)}, u32[]{:S(2)}, u32[]{:S(2)}) collective-permute-start(f32[2,8,128]{2,1,0:T(8,128)} %get-tuple-element.13.own_maps), channel_id=1, source_target_pairs={{0,256},{256,0},{1,257},{257,1},{2,258},{258,2},{3,259},{259,3},{4... | collective-permute-start | bytes 24584 | tf_op jit(solution)/shard_map/ppermute | solution.py:262
  27.6 0.6 copy-start.4
  28.2 0.7 copy-start.3
  30.6 9.4 %copy-start.5 = (f32[128]{0:T(128)S(1)}, f32[128]{0:T(128)}, u32[]{:S(2)}) copy-start(f32[128]{0:T(128)} %param.7) | copy-start | bytes 1540
  30.6 22.3 %all-to-all-start = ((f32[16,40,128]{2,1,0:T(8,128)}), f32[16,40,128]{2,1,0:T(8,128)S(1)}, u32[]{:S(2)}, u32[]{:S(2)}) async-start(f32[16,40,128]{2,1,0:T(8,128)} %pack.1), calls=%async_computation | async-start | bytes 655360 | tf_op jit(solution)/shard_map/all_to_all | solution.py:266
  40.5 0.7 copy-start.6
  52.9 0.7 copy-start
  56.5 11.9 %all-to-all-start.1 = ((f32[16,16,128]{2,1,0:T(8,128)}), f32[16,16,128]{2,1,0:T(8,128)S(1)}, u32[]{:S(2)}, u32[]{:S(2)}) async-start(f32[16,16,128]{2,1,0:T(8,128)} %solve.1), calls=%async_computation.1 | async-start | bytes 262144 | tf_op jit(solution)/shard_map/all_to_all | solution.py:280
  68.4 14.1 %copy-start.1 = (f32[16,16,128]{2,1,0:T(8,128)}, f32[16,16,128]{2,1,0:T(8,128)S(1)}, u32[]{:S(2)}) copy-start(f32[16,16,128]{2,1,0:T(8,128)S(1)} %all-to-all-done.1) | copy-start | bytes 393220
  69.6 15.8 %all-to-all-start.2 = ((f32[16,1,128]{2,1,0:T(1,128)}), f32[16,1,128]{2,1,0:T(1,128)S(1)}, u32[]{:S(2)}, u32[]{:S(2)}) async-start(f32[16,1,128]{2,1,0:T(1,128)} %broadcast_in_dim.15), calls=%async_computation.2 | async-start | bytes 16384 | tf_op jit(solution)/shard_map/all_to_all | solution.py:284

commit v2 on v1

v2 whole, which is shorter than its diff:
```python
import jax
import jax.numpy as jnp
from jax import lax
from jax.experimental import pallas as pl
from jax.experimental.pallas import tpu as pltpu
from jax.sharding import Mesh, PartitionSpec as P

HALVES, RING, LEVELS, ROWS, CELLS, SLAB = 2, 16, 8, 128, 256, 8
SEGMENTS = 8
STEPS = CELLS // SEGMENTS
SENT = 24
BACK = 16

VMEM = pl.BlockSpec(memory_space=pltpu.VMEM)
SMEM = pl.BlockSpec(memory_space=pltpu.SMEM)


def lanes(shape):
    return lax.broadcasted_iota(jnp.int32, shape, len(shape) - 1)


def scan_segments(source, courant, put):
    growth = jnp.ones((SEGMENTS, ROWS), jnp.float32)
    offset = jnp.zeros((SEGMENTS, ROWS), jnp.float32)
    for step in range(STEPS):
        at = pl.ds(step, SEGMENTS, stride=STEPS)
        c = courant[at, :]
        inverse = 1.0 / (1.0 + c)
        factor = c * inverse
        total = source[at, :] + offset
        put(at, total * inverse, growth * inverse)
        offset = factor * total
        growth = growth * factor
    place = lax.broadcasted_iota(jnp.int32, (SEGMENTS, ROWS), 0)
    for stride in (1, 2, 4):
        inside = place >= stride
        offset = jnp.where(inside, growth * pltpu.roll(offset, stride, 0) + offset, offset)
        growth = jnp.where(inside, growth * pltpu.roll(growth, stride, 0), growth)
    entry_growth = jnp.where(place >= 1, pltpu.roll(growth, 1, 0), 1.0)
    entry_offset = jnp.where(place >= 1, pltpu.roll(offset, 1, 0), 0.0)
    return entry_growth, entry_offset, growth[-1:], offset[-1:]


def scan_kernel(tracer, courant, part, slope, entry, source_t, courant_t):
    def level(l, slot):
        source_t[slot] = tracer[l].T
        courant_t[slot] = courant[l].T

        def put(at, a, b):
            part[l, at, :] = a
            slope[l, at, :] = b

        g, o, _, _ = scan_segments(source_t.at[slot], courant_t.at[slot], put)
        entry[l, 0] = g
        entry[l, 1] = o

    def pair(i, carry):
        level(2 * i, 0)
        level(2 * i + 1, 1)
        return carry

    lax.fori_loop(0, LEVELS // 2, pair, 0)


def scan(tracer, courant):
    f32 = jnp.float32
    shape = jax.ShapeDtypeStruct
    return pl.pallas_call(
        scan_kernel,
        out_shape=(
            shape((LEVELS, CELLS, ROWS), f32),
            shape((LEVELS, CELLS, ROWS), f32),
            shape((LEVELS, 2, SEGMENTS, ROWS), f32),
        ),
        in_specs=[VMEM, VMEM],
        out_specs=(VMEM, VMEM, VMEM),
        scratch_shapes=[pltpu.VMEM((2, CELLS, ROWS), f32)] * 2,
        name="scan",
    )(tracer, courant)


def turn_kernel(part, slope, entry, part_out, slope_out, buffer):
    def level(l, slot):
        g, o = entry[l, 0], entry[l, 1]
        for step in range(STEPS):
            at = pl.ds(step, SEGMENTS, stride=STEPS)
            b = slope[l, at, :]
            buffer[slot, 0, at, :] = part[l, at, :] + b * o
            buffer[slot, 1, at, :] = b * g
        part_out[l] = buffer[slot, 0].T
        slope_out[l] = buffer[slot, 1].T

    def pair(i, carry):
        level(2 * i, 0)
        level(2 * i + 1, 1)
        return carry

    lax.fori_loop(0, LEVELS // 2, pair, 0)


def turn(part, slope, entry):
    shape = jax.ShapeDtypeStruct((LEVELS, ROWS, CELLS), jnp.float32)
    return pl.pallas_call(
        turn_kernel,
        out_shape=(shape, shape),
        in_specs=[VMEM, VMEM, VMEM],
        out_specs=(VMEM, VMEM),
        scratch_shapes=[pltpu.VMEM((2, 2, CELLS, ROWS), jnp.float32)],
        name="turn",
    )(part, slope, entry)


def merge(bit, early, late):
    clear = (lanes((8, 128)) >> bit) % 2 == 0
    step = 1 << bit
    first_g = jnp.where(clear, early[0], pltpu.roll(late[0], step, 1))
    first_o = jnp.where(clear, early[1], pltpu.roll(late[1], step, 1))
    then_g = jnp.where(clear, pltpu.roll(early[0], 128 - step, 1), late[0])
    then_o = jnp.where(clear, pltpu.roll(early[1], 128 - step, 1), late[1])
    return first_g * then_g, then_g * first_o + then_o


def merged(maps, bits):
    for bit in bits:
        maps = [merge(bit, maps[i], maps[i + 1]) for i in range(0, len(maps), 2)]
    return maps[0]


def pack_kernel(tracer, courant, sent, source, factor, slab, sems):
    copies = [
        (
            pltpu.make_async_copy(tracer.at[l], source.at[l], sems.at[0, l]),
            pltpu.make_async_copy(courant.at[l], factor.at[l], sems.at[1, l]),
        )
        for l in range(LEVELS)
    ]
    for pair in copies:
        for copy in pair:
            copy.start()
    last = lax.axis_index("lat") == lax.axis_size("lat") - 1
    start = pl.multiple_of(jnp.where(last, ROWS - SLAB, 0), SLAB)
    sides = ([], [])
    for l in range(LEVELS):
        for copy in copies[l]:
            copy.wait()
        for side in range(2):
            across = pl.ds(128 * side, 128)
            maps = []
            for m in range(ROWS // 8):
                c = factor[l, pl.ds(8 * m, 8), across]
                f = c * (1.0 / (1.0 + c))
                maps.append((f, f * source[l, pl.ds(8 * m, 8), across]))
            sides[side].append(merged(maps, range(4)))
            slab[side, pl.ds(SLAB * l, SLAB), :] = source[l, pl.ds(start, SLAB), across]
            slab[2 + side, pl.ds(SLAB * l, SLAB), :] = factor[l, pl.ds(start, SLAB), across]
    west, east = merged(sides[0], range(4, 7)), merged(sides[1], range(4, 7))
    g, o = west[0] * east[0], east[0] * west[1] + east[1]
    low = lanes((8, 128)) < 64
    rows = (jnp.where(low, g, pltpu.roll(o, 64, 1)), jnp.where(low, pltpu.roll(g, 64, 1), o))
    zeros = jnp.zeros((SENT - 16, 128), jnp.float32)
    for r in range(SLAB):
        for a in range(4):
            x = slab[a, pl.ds(r, LEVELS, stride=SLAB), :]
            sent[2 * r, pl.ds(4 * a, 4), :] = x[:4]
            sent[2 * r + 1, pl.ds(4 * a, 4), :] = x[4:]
        for parity in range(2):
            sent[2 * r + parity, pl.ds(16, SENT - 16), :] = zeros
            sent[2 * r + parity, pl.ds(16, 1), :] = rows[parity][r : r + 1]


def pack(tracer, courant):
    f32 = jnp.float32
    return pl.pallas_call(
        pack_kernel,
        out_shape=pltpu.VMEM((RING, SENT, 128), f32),
        in_specs=[pl.BlockSpec(memory_space=pl.ANY)] * 2,
        out_specs=VMEM,
        scratch_shapes=[
            pltpu.VMEM((LEVELS, ROWS, CELLS), f32),
            pltpu.VMEM((LEVELS, ROWS, CELLS), f32),
            pltpu.VMEM((4, LEVELS * SLAB, 128), f32),
            pltpu.SemaphoreType.DMA((2, LEVELS)),
        ],
        name="pack",
    )(tracer, courant)


def solve_kernel(hops, areas, own, far_slab, far_maps, back, source, courant, source_t, courant_t, part, slope):
    lat = lax.axis_index("lat")
    half = lax.axis_index("half")
    ring = lax.axis_index("ring")
    last = lat == lax.axis_size("lat") - 1
    polar = (lat == 0) | last
    start = jnp.where(last, ROWS - SLAB, 0)
    row, parity = ring // 2, ring % 2
    for d in range(HALVES * RING):
        ref, base = (own, d * SENT) if d < RING else (far_slab, (d - RING) * 16)
        for side in range(2):
            to = pl.ds(side * 128, 128)
            source[pl.ds(4 * d, 4), to] = ref[pl.ds(base + 4 * side, 4), :]
            courant[pl.ds(4 * d, 4), to] = ref[pl.ds(base + 8 + 4 * side, 4), :]
    source_t[...] = pltpu.roll(source[...].T, 4 * hops[start + row], 1)
    courant_t[...] = courant[...].T

    def put(at, a, b):
        part[at, :] = a
        slope[at, :] = b

    entry_g, entry_o, g, o = scan_segments(source_t, courant_t, put)
    for stride in (4, 8, 16, 32, 64):
        o = g * pltpu.roll(o, stride, 1) + o
        g = g * pltpu.roll(g, stride, 1)
    inflow = pltpu.roll(o / (1.0 - g), 4, 1)
    entry = entry_g * inflow + entry_o
    for step in range(STEPS):
        at = pl.ds(step, SEGMENTS, stride=STEPS)
        source_t[at, :] = part[at, :] + slope[at, :] * entry
    source[...] = source_t[...].T
    x = jnp.concatenate([own[pl.ds(16, RING, stride=SENT), :], far_maps[...]], 0)
    low = lanes(x.shape) < 64
    turned = pltpu.roll(x, 64, 1)
    rest_g = jnp.where(low, x, turned)
    rest_o = jnp.where(low, turned, x)
    for stride in (1, 2, 4, 8, 16):
        rest_o = rest_g * pltpu.roll(rest_o, stride, 0) + rest_o
        rest_g = rest_g * pltpu.roll(rest_g, stride, 0)
    rest = pltpu.roll(rest_o / (1.0 - rest_g), 1, 0)
    wrap = jnp.where(half == 0, rest[:1], rest[RING : RING + 1])
    lane = lanes((1, 128))
    from_slab = polar & (lane % 16 == start // SLAB)
    weighted = jnp.where((lane // 64 == parity) & ~from_slab, wrap * areas[pl.ds(row, 1), :], 0.0)
    loops = pltpu.roll(inflow, 64 * ((parity + half) % 2), 1)
    area = jnp.sum(jnp.where(lane == start // SLAB, areas[pl.ds(row, 1), :], 0.0), axis=1, keepdims=True)
    for q in range(4):
        moved = pltpu.roll(loops, 15 * q, 1) if q else loops
        weighted = weighted + jnp.where(polar & (lane == 64 * parity + 16 * q), moved * area, 0.0)
    zeros = jnp.zeros((BACK - 8, 128), jnp.float32)
    for d in range(RING):
        for side in range(2):
            back[d, pl.ds(4 * side, 4), :] = source[pl.ds(4 * d, 4), pl.ds(side * 128, 128)]
        back[d, pl.ds(8, BACK - 8), :] = zeros
        back[d, pl.ds(8, 1), :] = rest[d : d + 1]
        back[d, pl.ds(9, 1), :] = weighted


def solve(hops, areas, own, far_slab, far_maps):
    f32 = jnp.float32
    return pl.pallas_call(
        solve_kernel,
        out_shape=pltpu.VMEM((RING, BACK, 128), f32),
        in_specs=[SMEM] + [VMEM] * 4,
        out_specs=VMEM,
        scratch_shapes=[pltpu.VMEM((ROWS, CELLS), f32)] * 2 + [pltpu.VMEM((CELLS, ROWS), f32)] * 4,
        name="solve",
    )(hops, areas, *[pltpu.with_memory_space_constraint(x, pltpu.VMEM) for x in (own, far_slab, far_maps)])


def spread_kernel(got, area, sums):
    total = jnp.sum(got[pl.ds(9, RING, stride=BACK), :], axis=0, keepdims=True)
    lane = lanes((1, 128))
    total = total + pltpu.roll(total, 120, 1)
    total = jnp.where(lane == 8, jnp.sum(area[...], axis=1, keepdims=True), total)
    for i in range(sums.shape[0]):
        sums[i] = total


def spread(got, area, lats):
    return pl.pallas_call(
        spread_kernel,
        out_shape=jax.ShapeDtypeStruct((lats, 1, 128), jnp.float32),
        in_specs=[VMEM, VMEM],
        out_specs=VMEM,
        name="spread",
    )(pltpu.with_memory_space_constraint(got, pltpu.VMEM), area)


def finish_kernel(part, slope, got, updated):
    low = lanes((8, 128)) < 64
    even = got[pl.ds(8, 8, stride=2 * BACK), :]
    odd = got[pl.ds(8 + BACK, 8, stride=2 * BACK), :]
    inflow = jnp.where(low, even, pltpu.roll(odd, 64, 1))
    for l in range(LEVELS):
        for m in range(ROWS // 8):
            at = pl.ds(8 * m, 8)
            lane = 16 * l + m
            updated[l, at, :] = part[l, at, :] + slope[l, at, :] * inflow[:, lane : lane + 1]
    lat = lax.axis_index("lat")
    last = lat == lax.axis_size("lat") - 1

    @pl.when((lat == 0) | last)
    def _():
        rows = pl.ds(pl.multiple_of(jnp.where(last, ROWS - SLAB, 0), SLAB), SLAB)
        for l in range(LEVELS):
            for side in range(2):
                at = (l // 4) * BACK + 4 * side + l % 4
                updated[l, rows, pl.ds(side * 128, 128)] = got[pl.ds(at, SLAB, stride=2 * BACK), :]


def finish(part, slope, got):
    return pl.pallas_call(
        finish_kernel,
        out_shape=jax.ShapeDtypeStruct((LEVELS, ROWS, CELLS), jnp.float32),
        in_specs=[VMEM, VMEM, VMEM],
        out_specs=VMEM,
        name="finish",
    )(part, slope, pltpu.with_memory_space_constraint(got, pltpu.VMEM))


def mean_kernel(sums, mean):
    total = sums[0]
    for i in range(1, sums.shape[0]):
        total = total + sums[i]
    lane = lanes((1, 128))
    area = jnp.sum(jnp.where(lane == 8, total, 0.0), axis=1, keepdims=True)
    for step in (4, 2, 1):
        total = total + pltpu.roll(total, 128 - step, 1)
    levels = total
    for l in range(1, LEVELS):
        levels = jnp.where(lane == l, pltpu.roll(total, 128 - 15 * l, 1), levels)
    mean[...] = (levels / area)[0, :LEVELS]


def mean(sums):
    return pl.pallas_call(
        mean_kernel,
        out_shape=jax.ShapeDtypeStruct((LEVELS,), jnp.float32),
        in_specs=[VMEM],
        out_specs=VMEM,
        name="mean",
    )(pltpu.with_memory_space_constraint(sums, pltpu.VMEM))


def body(tracer, courant, hop_counts, row_area):
    lats = lax.axis_size("lat")

    def across(i):
        h, rest = divmod(i, RING * lats)
        moved = rest % lats in (0, lats - 1)
        return (i, (1 - h) * RING * lats + rest if moved else i)

    sent = pack(tracer, courant)
    got = lax.all_to_all(sent, "ring", 0, 0, tiled=True)
    every = ("half", "ring", "lat")
    far_slab = lax.ppermute(got[:, :16], every, [across(i) for i in range(HALVES * RING * lats)])
    far_maps = lax.ppermute(got[:, 16], "half", [(0, 1), (1, 0)])
    tracer, courant, got = lax.optimization_barrier((tracer, courant, got))
    scanned = scan(tracer, courant)
    scanned, far_slab = lax.optimization_barrier((scanned, far_slab))
    part, slope = turn(*scanned)
    areas = jnp.tile(row_area.reshape(ROWS // 8, 8).T, (1, 8))
    back = solve(
        hop_counts, areas, got.reshape(RING * SENT, 128), far_slab.reshape(RING * 16, 128), far_maps
    )
    back = lax.all_to_all(back, "ring", 0, 0, tiled=True).reshape(RING * BACK, 128)
    sums = lax.all_to_all(spread(back, row_area.reshape(1, ROWS), lats), "lat", 0, 0, tiled=True)
    return finish(part, slope, back), mean(sums)


def solution(mesh):
    split = Mesh(mesh.devices.reshape(HALVES, RING, -1), ("half", "ring", "lat"))
    field = P(None, "lat", ("half", "ring"))
    return jax.shard_map(
        body,
        mesh=split,
        in_specs=(field, field, P("lat"), P("lat")),
        out_specs=(field, P()),
        check_vma=False,
    )
```

time: 87.7 us -> 75.3 us (0.86)
  blocking collectives: 0 us -> 32.3 us
  waiting for transfers between devices: 23.4 us -> 0.01 us
  starting transfers between devices: 32.7 us -> 18.2 us
  local copies, waits for them, and re-layouts: 6.08 us -> 0.86 us
  other arithmetic: 4.26 us -> 0 us
  Pallas kernels: 19.3 us -> 22.8 us
    all_to_all x0 -> x2, blocking collectives: none -> 32.3 us  [the longest x1 19.5 us: body(): got = lax.all_to_all(sent, 'ring', 0, 0, tiled=True)]
    all_to_all x3 -> x1, waiting for transfers between devices: 16.8 us -> 0.01 us  [body(): lax.all_to_all(spread(back, row_area.reshape(1, ROWS), lats), 'lat', 0, 0...]
    all_to_all x3 -> x1, starting transfers between devices: 19.3 us -> 6.59 us  [body(): lax.all_to_all(spread(back, row_area.reshape(1, ROWS), lats), 'lat', 0, 0...]
    ppermute x2, waiting for transfers between devices: 6.58 us -> 0.01 us  [the longest x1 0.01 us: body(): lax.ppermute(got[:, :16], every, [across(i) for i in range(HALVES * RING...]
    pallas_call x3 -> x5, Pallas kernels: 10.7 us -> 14.2 us  [the longest x1 5.76 us: scan(): pl.pallas_call(scan_kernel, out_shape=(shape((LEVELS, CELLS, ROWS), f32),...]
    unnamed x14 -> x2, local copies, waits for them, and re-layouts: 2.06 us -> 0.01 us
    another operation x4 -> x0, other arithmetic: 1.99 us -> none  [the longest x1 1.3 us: body(): scalars = jnp.stack([hop, half, row, parity]).astype(jnp.int32)]
    ppermute x2, starting transfers between devices: 13.4 us -> 11.6 us  [the longest x1 9.72 us: body(): lax.ppermute(got[:, :16], every, [across(i) for i in range(HALVES * RING...]
  transfers between devices with their start and end apart: 5 -> 3, of which waited for: 3 -> 0; matrix products, arithmetic and copies ran while one was open for 5% -> 1% of each run, Pallas kernels for 17% -> 19%
where the time goes in v2:
time: 75.3 us; the launch traced here: 74.9 us
  blocking collectives  32.3 us (43%)
  Pallas kernels  22.8 us (30%)
  starting transfers between devices  18.2 us (24%)
  local copies, waits for them, and re-layouts  0.86 us (1%)
    all_to_all x1, blocking collectives, body(): got = lax.all_to_all(sent, 'ring', 0, 0, tiled=True)  19.5 us
    all_to_all x1, blocking collectives, body(): lax.all_to_all(back, 'ring', 0, 0, tiled=True).reshape(RING * BACK, 128)  12.8 us
    ppermute x1, starting transfers between devices, body(): lax.ppermute(got[:, :16], every, [across(i) for i in range(HALVES * RING...  9.72 us
    all_to_all x1, starting transfers between devices, body(): lax.all_to_all(spread(back, row_area.reshape(1, ROWS), lats), 'lat', 0, 0...  6.59 us
    pallas_call x1, Pallas kernels, scan(): pl.pallas_call(scan_kernel, out_shape=(shape((LEVELS, CELLS, ROWS), f32),...  5.76 us
    pallas_call x1, Pallas kernels, turn(): pl.pallas_call(turn_kernel, out_shape=(shape, shape), in_specs=[VMEM, VME...  5.7 us
    pallas_call x1, Pallas kernels, pack(): pl.pallas_call(pack_kernel, out_shape=pltpu.VMEM((RING, SENT, 128), f32),...  4.34 us
    pallas_call x1, Pallas kernels, finish(): pl.pallas_call(finish_kernel, out_shape=jax.ShapeDtypeStruct((LEVELS, ROW...  2.9 us
  transfers between devices with their start and end apart: 3, of which 0 were waited for; matrix products, arithmetic and copies ran while one was open for 1% of the time, Pallas kernels for 19%

profile of v2, /device:TPU:1, one launch (start us, length us, event | category | flops | bytes accessed | tf_op | source)
XLA Modules:
  0.0 74.9 jit_solution(6913773236912356400)
XLA Ops:
  0.6 4.3 %pack.1 = f32[16,24,128]{2,1,0:T(8,128)S(1)} custom-call(f32[8,128,256]{2,1,0:T(8,128)} %tracer.2, f32[8,128,256]{2,1,0:T(8,128)} %courant.2), custom_call_target="tpu_custom_call" | custom-call | tf_op jit(solution)/shard_map/pack/pallas_call | solution.py:173
  5.0 19.5 %all_to_all.15 = f32[16,24,128]{2,1,0:T(8,128)S(1)} all-to-all(f32[16,24,128]{2,1,0:T(8,128)S(1)} %pack.1), channel_id=1, replica_groups=mesh['half'=2,'ring'=16,'lat'=16] {'ring'}, dimensions={0} | all-to-all | bytes 393216 | tf_op jit(solution)/shard_map/all_to_all | solution.py:342
  24.5 9.7 %collective-permute-start = (f32[16,16,128]{2,1,0:T(8,128)S(1)}, f32[16,16,128]{2,1,0:T(8,128)S(1)}, u32[]{:S(2)}, u32[]{:S(2)}) collective-permute-start(f32[16,16,128]{2,1,0:T(8,128)S(1)} %slice.8), channel_id=1, source_target_pairs={{0,256},{1,1},{2,2},{3,3},{4,4},{5,5},{6,6},{7,7},{8,8},{9,9},{10,... | collective-permute-start | bytes 393224 | tf_op jit(solution)/shard_map/ppermute | solution.py:344
  34.2 0.0 copy-start
  34.3 1.9 %collective-permute-start.1 = (f32[16,128]{1,0:T(8,128)S(1)}, f32[16,128]{1,0:T(8,128)S(1)}, u32[]{:S(2)}, u32[]{:S(2)}) collective-permute-start(f32[16,128]{1,0:T(8,128)S(1)} %bitcast.13), channel_id=1, source_target_pairs={{0,256},{256,0},{1,257},{257,1},{2,258},{258,2},{3,259},{259,3},{4... | collective-permute-start | bytes 24584 | tf_op jit(solution)/shard_map/ppermute | solution.py:345
  36.2 0.0 copy-done
  36.2 0.1 reshape.23
  36.3 0.1 copy.12
  36.4 0.7 tile.10.areas
  37.0 5.8 %scan.1 = (f32[8,256,128]{2,1,0:T(8,128)}, f32[8,256,128]{2,1,0:T(8,128)}, f32[8,2,8,128]{3,2,1,0:T(8,128)}) custom-call(f32[8,128,256]{2,1,0:T(8,128)} %tracer.2, f32[8,128,256]{2,1,0:T(8,128)} %courant.2), custom_call_target="tpu_custom_call" | custom-call | tf_op jit(solution)/shard_map/scan/pallas_call | solution.py:68
  42.8 0.0 collective-permute-done
  42.8 0.0 collective-permute-done.1.far_maps
  42.8 1.9 %solve.1 = f32[16,16,128]{2,1,0:T(8,128)S(1)} custom-call(s32[128]{0:T(128)} %hops.1, f32[8,128]{1,0:T(8,128)} %tile.10.areas, f32[384,128]{1,0:T(8,128)S(1)} %bitcast.8, f32[256,128]{1,0:T(8,128)S(1)} %bitcast.11, f32[16,128]{1,0:T(8,128)S(1)} %collective-permute-done.1.far_maps), custom_call_target="tpu_custom_call" | custom-call | tf_op jit(solution)/shard_map/solve/pallas_call | solution.py:248
  44.8 12.8 %all_to_all.16 = f32[16,16,128]{2,1,0:T(8,128)S(1)} all-to-all(f32[16,16,128]{2,1,0:T(8,128)S(1)} %solve.1), channel_id=1, replica_groups=mesh['half'=2,'ring'=16,'lat'=16] {'ring'}, dimensions={0} | all-to-all | bytes 262144 | tf_op jit(solution)/shard_map/all_to_all | solution.py:354
  57.6 1.3 %spread.1 = f32[16,1,128]{2,1,0:T(1,128)} custom-call(f32[256,128]{1,0:T(8,128)S(1)} %bitcast.9, f32[1,128]{1,0:T(1,128)} %bitcast.14), custom_call_target="tpu_custom_call" | custom-call | tf_op jit(solution)/shard_map/spread/pallas_call | solution.py:268
  58.9 6.6 %all-to-all-start.2 = ((f32[16,1,128]{2,1,0:T(1,128)}), f32[16,1,128]{2,1,0:T(1,128)S(1)}, u32[]{:S(2)}, u32[]{:S(2)}) async-start(f32[16,1,128]{2,1,0:T(1,128)} %spread.1), calls=%async_computation.2 | async-start | bytes 16384 | tf_op jit(solution)/shard_map/all_to_all | solution.py:355
  65.5 5.7 %turn.1 = (f32[8,128,256]{2,1,0:T(8,128)}, f32[8,128,256]{2,1,0:T(8,128)}) custom-call(f32[8,256,128]{2,1,0:T(8,128)} %get-tuple-element.19.part, f32[8,256,128]{2,1,0:T(8,128)} %get-tuple-element.20.slope, f32[8,2,8,128]{3,2,1,0:T(8,128)} %get-tuple-element.21.entry), custom_call_target="tpu_custom_call" | custom-call | tf_op jit(solution)/shard_map/turn/pallas_call | solution.py:103
  71.2 2.9 %finish.1 = f32[8,128,256]{2,1,0:T(8,128)} custom-call(f32[8,128,256]{2,1,0:T(8,128)} %get-tuple-element.22.part, f32[8,128,256]{2,1,0:T(8,128)} %get-tuple-element.23.slope, f32[256,128]{1,0:T(8,128)S(1)} %bitcast.10), custom_call_target="tpu_custom_call" | custom-call | tf_op jit(solution)/shard_map/finish/pallas_call | solution.py:300
  74.1 0.0 all-to-all-done.2.sums
  74.1 0.8 %mean.1 = f32[8]{0:T(128)} custom-call(f32[16,1,128]{2,1,0:T(1,128)S(1)} %all-to-all-done.2.sums), custom_call_target="tpu_custom_call" | custom-call | tf_op jit(solution)/shard_map/mean/pallas_call | solution.py:324
  (3 shorter events, 0.0 us)
Async XLA Ops:
  24.5 18.3 %collective-permute-start = (f32[16,16,128]{2,1,0:T(8,128)S(1)}, f32[16,16,128]{2,1,0:T(8,128)S(1)}, u32[]{:S(2)}, u32[]{:S(2)}) collective-permute-start(f32[16,16,128]{2,1,0:T(8,128)S(1)} %slice.8), channel_id=1, source_target_pairs={{0,256},{1,1},{2,2},{3,3},{4,4},{5,5},{6,6},{7,7},{8,8},{9,9},{10,... | collective-permute-start | bytes 393224 | tf_op jit(solution)/shard_map/ppermute | solution.py:344
  34.2 1.9 %copy-start = (f32[128]{0:T(128)S(1)}, f32[128]{0:T(128)}, u32[]{:S(2)}) copy-start(f32[128]{0:T(128)} %param.7) | copy-start | bytes 1540
  34.3 8.6 %collective-permute-start.1 = (f32[16,128]{1,0:T(8,128)S(1)}, f32[16,128]{1,0:T(8,128)S(1)}, u32[]{:S(2)}, u32[]{:S(2)}) collective-permute-start(f32[16,128]{1,0:T(8,128)S(1)} %bitcast.13), channel_id=1, source_target_pairs={{0,256},{256,0},{1,257},{257,1},{2,258},{258,2},{3,259},{259,3},{4... | collective-permute-start | bytes 24584 | tf_op jit(solution)/shard_map/ppermute | solution.py:345
  58.9 15.2 %all-to-all-start.2 = ((f32[16,1,128]{2,1,0:T(1,128)}), f32[16,1,128]{2,1,0:T(1,128)S(1)}, u32[]{:S(2)}, u32[]{:S(2)}) async-start(f32[16,1,128]{2,1,0:T(1,128)} %spread.1), calls=%async_computation.2 | async-start | bytes 16384 | tf_op jit(solution)/shard_map/all_to_all | solution.py:355

commit v3 on v2

v3 whole, which is shorter than its diff:
```python
import jax
import jax.numpy as jnp
from jax import lax
from jax.experimental import pallas as pl
from jax.experimental.pallas import tpu as pltpu
from jax.sharding import Mesh, PartitionSpec as P

HALVES, RING, LEVELS, ROWS, CELLS, SLAB = 2, 16, 8, 128, 256, 8
SEGMENTS = 8
STEPS = CELLS // SEGMENTS
SENT = 24
BACK = 16

VMEM = pl.BlockSpec(memory_space=pltpu.VMEM)
SMEM = pl.BlockSpec(memory_space=pltpu.SMEM)


def lanes(shape):
    return lax.broadcasted_iota(jnp.int32, shape, len(shape) - 1)


def polar_start():
    lat = lax.axis_index("lat")
    last = lat == lax.axis_size("lat") - 1
    return (lat == 0) | last, pl.multiple_of(jnp.where(last, ROWS - SLAB, 0), SLAB)


def in_vmem(*arrays):
    return [pltpu.with_memory_space_constraint(x, pltpu.VMEM) for x in arrays]


def pack_kernel(tracer, courant, sent, source_t, courant_t, entries, source, factor, slab, sems):
    copies = [
        (
            pltpu.make_async_copy(tracer.at[l], source.at[l], sems.at[0, l]),
            pltpu.make_async_copy(courant.at[l], factor.at[l], sems.at[1, l]),
        )
        for l in range(LEVELS)
    ]
    for pair in copies:
        for copy in pair:
            copy.start()
    _, start = polar_start()
    for l in range(LEVELS):
        for copy in copies[l]:
            copy.wait()
        source_t[pl.ds(l, CELLS, stride=LEVELS), :] = source[l].T
        courant_t[pl.ds(l, CELLS, stride=LEVELS), :] = factor[l].T
        for side in range(2):
            across = pl.ds(128 * side, 128)
            slab[side, pl.ds(SLAB * l, SLAB), :] = source[l, pl.ds(start, SLAB), across]
            slab[2 + side, pl.ds(SLAB * l, SLAB), :] = factor[l, pl.ds(start, SLAB), across]
    growth = [jnp.ones((LEVELS, ROWS), jnp.float32)] * SEGMENTS
    offset = [jnp.zeros((LEVELS, ROWS), jnp.float32)] * SEGMENTS
    for step in range(STEPS):
        for k in range(SEGMENTS):
            at = pl.ds(LEVELS * (STEPS * k + step), LEVELS)
            c = courant_t[at, :]
            f = c * (1.0 / (1.0 + c))
            offset[k] = f * (source_t[at, :] + offset[k])
            growth[k] = growth[k] * f
    g, o = growth[0], offset[0]
    for k in range(1, SEGMENTS):
        entries[2 * k] = g
        entries[2 * k + 1] = o
        g, o = g * growth[k], growth[k] * o + offset[k]
    low = lanes((LEVELS, ROWS)) < 64
    maps = (jnp.where(low, g, pltpu.roll(o, 64, 1)), jnp.where(low, pltpu.roll(g, 64, 1), o))
    zeros = jnp.zeros((SENT - 16, 128), jnp.float32)
    for r in range(SLAB):
        for a in range(4):
            x = slab[a, pl.ds(r, LEVELS, stride=SLAB), :]
            sent[2 * r, pl.ds(4 * a, 4), :] = x[:4]
            sent[2 * r + 1, pl.ds(4 * a, 4), :] = x[4:]
        for parity in range(2):
            sent[2 * r + parity, pl.ds(16, SENT - 16), :] = zeros
            sent[2 * r + parity, pl.ds(16, 1), :] = maps[parity][r : r + 1]


def pack(tracer, courant):
    f32 = jnp.float32
    return pl.pallas_call(
        pack_kernel,
        out_shape=(
            pltpu.VMEM((RING, SENT, 128), f32),
            pltpu.VMEM((CELLS * LEVELS, ROWS), f32),
            pltpu.VMEM((CELLS * LEVELS, ROWS), f32),
            pltpu.VMEM((2 * SEGMENTS, LEVELS, ROWS), f32),
        ),
        in_specs=[pl.BlockSpec(memory_space=pl.ANY)] * 2,
        out_specs=(VMEM,) * 4,
        scratch_shapes=[
            pltpu.VMEM((LEVELS, ROWS, CELLS), f32),
            pltpu.VMEM((LEVELS, ROWS, CELLS), f32),
            pltpu.VMEM((4, LEVELS * SLAB, 128), f32),
            pltpu.SemaphoreType.DMA((2, LEVELS)),
        ],
        name="pack",
    )(tracer, courant)


def solve_kernel(hops, area, own, far_slab, far_maps, back, source, courant, source_t, courant_t):
    half = lax.axis_index("half")
    ring = lax.axis_index("ring")
    polar, start = polar_start()
    row, parity = ring // 2, ring % 2
    for d in range(HALVES * RING):
        ref, base = (own, d * SENT) if d < RING else (far_slab, (d - RING) * 16)
        for side in range(2):
            to = pl.ds(side * 128, 128)
            source[pl.ds(4 * d, 4), to] = ref[pl.ds(base + 4 * side, 4), :]
            courant[pl.ds(4 * d, 4), to] = ref[pl.ds(base + 8 + 4 * side, 4), :]
    source_t[...] = pltpu.roll(source[...].T, 4 * hops[start + row], 1)
    courant_t[...] = courant[...].T
    parts = range(CELLS // 64)
    growth = [jnp.ones((8, ROWS), jnp.float32) for k in parts]
    offset = [jnp.zeros((8, ROWS), jnp.float32) for k in parts]
    for step in range(8):
        for k in parts:
            at = pl.ds(64 * k + step, 8, stride=8)
            c = courant_t[at, :]
            f = c * (1.0 / (1.0 + c))
            offset[k] = f * (source_t[at, :] + offset[k])
            growth[k] = growth[k] * f
    place = lax.broadcasted_iota(jnp.int32, (8, ROWS), 0)
    for stride in (1, 2, 4):
        inside = place >= stride
        for k in parts:
            offset[k] = jnp.where(inside, growth[k] * pltpu.roll(offset[k], stride, 0) + offset[k], offset[k])
            growth[k] = jnp.where(inside, growth[k] * pltpu.roll(growth[k], stride, 0), growth[k])
    g = jnp.ones((1, ROWS), jnp.float32)
    o = jnp.zeros((1, ROWS), jnp.float32)
    entry = []
    for k in parts:
        first = place == 0
        before_g = jnp.where(first, 1.0, pltpu.roll(growth[k], 1, 0))
        before_o = jnp.where(first, 0.0, pltpu.roll(offset[k], 1, 0))
        entry.append((before_g * g, before_g * o + before_o))
        g, o = g * growth[k][7:], growth[k][7:] * o + offset[k][7:]
    for stride in (4, 8, 16, 32, 64):
        o = g * pltpu.roll(o, stride, 1) + o
        g = g * pltpu.roll(g, stride, 1)
    inflow = pltpu.roll(o / (1.0 - g), 4, 1)
    flux = [entry[k][0] * inflow + entry[k][1] for k in parts]
    for step in range(8):
        for k in parts:
            at = pl.ds(64 * k + step, 8, stride=8)
            c = courant_t[at, :]
            u = (source_t[at, :] + flux[k]) * (1.0 / (1.0 + c))
            source_t[at, :] = u
            flux[k] = c * u
    source[...] = source_t[...].T
    x = jnp.concatenate([own[pl.ds(16, RING, stride=SENT), :], far_maps[...]], 0)
    low = lanes(x.shape) < 64
    turned = pltpu.roll(x, 64, 1)
    rest_g = jnp.where(low, x, turned)
    rest_o = jnp.where(low, turned, x)
    for stride in (1, 2, 4, 8, 16):
        rest_o = rest_g * pltpu.roll(rest_o, stride, 0) + rest_o
        rest_g = rest_g * pltpu.roll(rest_g, stride, 0)
    rest = pltpu.roll(rest_o / (1.0 - rest_g), 1, 0)
    wrap = jnp.where(half == 0, rest[:1], rest[RING : RING + 1])
    lane = lanes((1, 128))
    areas = area[...]
    mine = lane // 64 == parity
    in_slab = polar & (lane >= start) & (lane < start + SLAB)
    weighted = jnp.where(mine & ~in_slab, areas, 0.0) * wrap
    weighted = jnp.sum(weighted, axis=1, keepdims=True)
    slab_area = jnp.sum(jnp.where(polar & (lane == start + row), areas, 0.0), axis=1, keepdims=True)
    loops = pltpu.roll(inflow, (4 * parity + 128 - 64 * half) % 128, 1) * slab_area
    sums = jnp.where(lane == row, weighted, 0.0)
    sums = sums + jnp.where((lane >= 4 * parity) & (lane < 4 * parity + 4), loops, 0.0)
    total = jnp.sum(areas, axis=1, keepdims=True)
    sums = jnp.where(lane == 8, jnp.where(ring == 0, total, 0.0), sums)
    zeros = jnp.zeros((BACK - 8, 128), jnp.float32)
    for d in range(RING):
        for side in range(2):
            back[d, pl.ds(4 * side, 4), :] = source[pl.ds(4 * d, 4), pl.ds(side * 128, 128)]
        back[d, pl.ds(8, BACK - 8), :] = zeros
        back[d, pl.ds(8, 1), :] = rest[d : d + 1]
        back[d, pl.ds(9, 1), :] = sums


def solve(hops, area, own, far_slab, far_maps):
    f32 = jnp.float32
    return pl.pallas_call(
        solve_kernel,
        out_shape=pltpu.VMEM((RING, BACK, 128), f32),
        in_specs=[SMEM] + [VMEM] * 4,
        out_specs=VMEM,
        scratch_shapes=[pltpu.VMEM((ROWS, CELLS), f32)] * 2 + [pltpu.VMEM((CELLS, ROWS), f32)] * 2,
        name="solve",
    )(hops, area, *in_vmem(own, far_slab, far_maps))


def spread_kernel(got, sums):
    total = jnp.sum(got[pl.ds(9, RING, stride=BACK), :], axis=0, keepdims=True)
    for i in range(sums.shape[0]):
        sums[i] = total


def spread(got, lats):
    return pl.pallas_call(
        spread_kernel,
        out_shape=jax.ShapeDtypeStruct((lats, 1, 128), jnp.float32),
        in_specs=[VMEM],
        out_specs=VMEM,
        name="spread",
    )(*in_vmem(got))


def finish_kernel(source_t, courant_t, entries, got, updated, updated_t):
    low = lanes((LEVELS, ROWS)) < 64
    even = got[pl.ds(8, LEVELS, stride=2 * BACK), :]
    odd = got[pl.ds(8 + BACK, LEVELS, stride=2 * BACK), :]
    inflow = jnp.where(low, even, odd)
    flux = [inflow] + [entries[2 * k] * inflow + entries[2 * k + 1] for k in range(1, SEGMENTS)]
    for step in range(STEPS):
        for k in range(SEGMENTS):
            at = pl.ds(LEVELS * (STEPS * k + step), LEVELS)
            c = courant_t[at, :]
            u = (source_t[at, :] + flux[k]) * (1.0 / (1.0 + c))
            updated_t[at, :] = u
            flux[k] = c * u
    for l in range(LEVELS):
        updated[l] = updated_t[pl.ds(l, CELLS, stride=LEVELS), :].T
    polar, start = polar_start()

    @pl.when(polar)
    def _():
        rows = pl.ds(start, SLAB)
        for l in range(LEVELS):
            for side in range(2):
                at = (l // 4) * BACK + 4 * side + l % 4
                updated[l, rows, pl.ds(side * 128, 128)] = got[pl.ds(at, SLAB, stride=2 * BACK), :]


def finish(source_t, courant_t, entries, got):
    return pl.pallas_call(
        finish_kernel,
        out_shape=jax.ShapeDtypeStruct((LEVELS, ROWS, CELLS), jnp.float32),
        in_specs=[VMEM] * 4,
        out_specs=VMEM,
        scratch_shapes=[pltpu.VMEM((CELLS * LEVELS, ROWS), jnp.float32)],
        name="finish",
    )(*in_vmem(source_t, courant_t, entries, got))


def mean_kernel(sums, mean):
    total = sums[0]
    for i in range(1, sums.shape[0]):
        total = total + sums[i]
    area = jnp.sum(jnp.where(lanes((1, 128)) == 8, total, 0.0), axis=1, keepdims=True)
    mean[...] = (total / area)[0, :LEVELS]


def mean(sums):
    return pl.pallas_call(
        mean_kernel,
        out_shape=jax.ShapeDtypeStruct((LEVELS,), jnp.float32),
        in_specs=[VMEM],
        out_specs=VMEM,
        name="mean",
    )(*in_vmem(sums))


def body(tracer, courant, hop_counts, row_area):
    lats = lax.axis_size("lat")

    def across(i):
        h, rest = divmod(i, RING * lats)
        moved = rest % lats in (0, lats - 1)
        return (i, (1 - h) * RING * lats + rest if moved else i)

    sent, source_t, courant_t, entries = pack(tracer, courant)
    got = lax.all_to_all(sent, "ring", 0, 0, tiled=True)
    every = ("half", "ring", "lat")
    far_slab = lax.ppermute(got[:, :16], every, [across(i) for i in range(HALVES * RING * lats)])
    far_maps = lax.ppermute(got[:, 16], "half", [(0, 1), (1, 0)])
    back = solve(
        hop_counts,
        row_area.reshape(1, ROWS),
        got.reshape(RING * SENT, 128),
        far_slab.reshape(RING * 16, 128),
        far_maps,
    )
    back = lax.all_to_all(back, "ring", 0, 0, tiled=True).reshape(RING * BACK, 128)
    sums = lax.all_to_all(spread(back, lats), "lat", 0, 0, tiled=True)
    return finish(source_t, courant_t, entries, back), mean(sums)


def solution(mesh):
    split = Mesh(mesh.devices.reshape(HALVES, RING, -1), ("half", "ring", "lat"))
    field = P(None, "lat", ("half", "ring"))
    return jax.shard_map(
        body,
        mesh=split,
        in_specs=(field, field, P("lat"), P("lat")),
        out_specs=(field, P()),
        check_vma=False,
    )
```

time: 75.3 us -> 70.2 us (0.932)
  Pallas kernels: 22.8 us -> 6.83 us
  waiting for transfers between devices: 0.01 us -> 11.6 us
  local copies, waits for them, and re-layouts: 0.86 us -> 0.02 us
    pallas_call x3 -> x1, Pallas kernels: 15.8 us -> 2.48 us  [pack(): pl.pallas_call(pack_kernel, out_shape=(pltpu.VMEM((RING, SENT, 128), f32)...]
    ppermute x1, waiting for transfers between devices: 0.01 us -> 6.37 us  [body(): far_maps = lax.ppermute(got[:, 16], 'half', [(0, 1), (1, 0)])]
    all_to_all x1, waiting for transfers between devices: 0.01 us -> 5.22 us  [body(): sums = lax.all_to_all(spread(back, lats), 'lat', 0, 0, tiled=True)]
    pallas_call x1, Pallas kernels: 2.9 us -> 1.57 us  [finish(): pl.pallas_call(finish_kernel, out_shape=jax.ShapeDtypeStruct((LEVELS, ROW...]
  transfers between devices with their start and end apart: 3 -> 3, of which waited for: 0 -> 2; matrix products, arithmetic and copies ran while one was open for 1% -> 0% of each run, Pallas kernels for 19% -> 2%
where the time goes in v3:
time: 70.2 us; the launch traced here: 69.9 us
  blocking collectives  32.6 us (46%)
  starting transfers between devices  18.2 us (26%)
  waiting for transfers between devices  11.6 us (17%)
  Pallas kernels  6.83 us (10%)
    all_to_all x1, blocking collectives, body(): got = lax.all_to_all(sent, 'ring', 0, 0, tiled=True)  19.5 us
    all_to_all x1, blocking collectives, body(): lax.all_to_all(back, 'ring', 0, 0, tiled=True).reshape(RING * BACK, 128)  13.1 us
    ppermute x1, starting transfers between devices, body(): lax.ppermute(got[:, :16], every, [across(i) for i in range(HALVES * RING...  9.72 us
    all_to_all x1, starting transfers between devices, body(): sums = lax.all_to_all(spread(back, lats), 'lat', 0, 0, tiled=True)  6.59 us
    ppermute x1, waiting for transfers between devices, body(): far_maps = lax.ppermute(got[:, 16], 'half', [(0, 1), (1, 0)])  6.37 us
    all_to_all x1, waiting for transfers between devices, body(): sums = lax.all_to_all(spread(back, lats), 'lat', 0, 0, tiled=True)  5.22 us
    pallas_call x1, Pallas kernels, pack(): pl.pallas_call(pack_kernel, out_shape=(pltpu.VMEM((RING, SENT, 128), f32)...  2.48 us
    ppermute x1, starting transfers between devices, body(): far_maps = lax.ppermute(got[:, 16], 'half', [(0, 1), (1, 0)])  1.92 us
  transfers between devices with their start and end apart: 3, of which 2 were waited for; matrix products, arithmetic and copies ran while one was open for 0% of the time, Pallas kernels for 2%

profile of v3, /device:TPU:1, one launch (start us, length us, event | category | flops | bytes accessed | tf_op | source)
XLA Modules:
  0.0 69.9 jit_solution(149131991706321591)
XLA Ops:
  0.6 2.5 %pack.1 = (f32[16,24,128]{2,1,0:T(8,128)S(1)}, f32[2048,128]{1,0:T(8,128)S(1)}, f32[2048,128]{1,0:T(8,128)S(1)}, f32[16,8,128]{2,1,0:T(8,128)S(1)}) custom-call(f32[8,128,256]{2,1,0:T(8,128)} %tracer.1, f32[8,128,256]{2,1,0:T(8,128)} %courant.1), custom_call_target="tpu_custom_call" | custom-call | tf_op jit(solution)/shard_map/pack/pallas_call | solution.py:82
  3.1 19.5 %all_to_all.15 = f32[16,24,128]{2,1,0:T(8,128)S(1)} all-to-all(f32[16,24,128]{2,1,0:T(8,128)S(1)} %get-tuple-element.9), channel_id=1, replica_groups=mesh['half'=2,'ring'=16,'lat'=16] {'ring'}, dimensions={0} | all-to-all | bytes 393216 | tf_op jit(solution)/shard_map/all_to_all | solution.py:276
  22.7 9.7 %collective-permute-start = (f32[16,16,128]{2,1,0:T(8,128)S(1)}, f32[16,16,128]{2,1,0:T(8,128)S(1)}, u32[]{:S(2)}, u32[]{:S(2)}) collective-permute-start(f32[16,16,128]{2,1,0:T(8,128)S(1)} %slice.8), channel_id=1, source_target_pairs={{0,256},{1,1},{2,2},{3,3},{4,4},{5,5},{6,6},{7,7},{8,8},{9,9},{10,... | collective-permute-start | bytes 393224 | tf_op jit(solution)/shard_map/ppermute | solution.py:278
  32.4 1.9 %collective-permute-start.1 = (f32[16,128]{1,0:T(8,128)S(1)}, f32[16,128]{1,0:T(8,128)S(1)}, u32[]{:S(2)}, u32[]{:S(2)}) collective-permute-start(f32[16,128]{1,0:T(8,128)S(1)} %bitcast.11), channel_id=1, source_target_pairs={{0,256},{256,0},{1,257},{257,1},{2,258},{258,2},{3,259},{259,3},{4... | collective-permute-start | bytes 24584 | tf_op jit(solution)/shard_map/ppermute | solution.py:279
  34.3 6.4 %collective-permute-done.1.far_maps = f32[16,128]{1,0:T(8,128)S(1)} collective-permute-done((f32[16,128]{1,0:T(8,128)S(1)}, f32[16,128]{1,0:T(8,128)S(1)}, u32[]{:S(2)}, u32[]{:S(2)}) %collective-permute-start.1) | collective-permute-done | bytes 8224 | tf_op jit(solution)/shard_map/ppermute | solution.py:279
  40.7 0.0 collective-permute-done
  40.7 1.6 %solve.1 = f32[16,16,128]{2,1,0:T(8,128)S(1)} custom-call(s32[128]{0:T(128)} %hops.1, f32[1,128]{1,0:T(1,128)} %bitcast.12, f32[384,128]{1,0:T(8,128)S(1)} %bitcast.7, f32[256,128]{1,0:T(8,128)S(1)} %bitcast.10, f32[16,128]{1,0:T(8,128)S(1)} %collective-permute-done.1.far_maps), custom_call_target="tpu_custom_call" | custom-call | tf_op jit(solution)/shard_map/solve/pallas_call | solution.py:186
  42.3 13.1 %all_to_all.16 = f32[16,16,128]{2,1,0:T(8,128)S(1)} all-to-all(f32[16,16,128]{2,1,0:T(8,128)S(1)} %solve.1), channel_id=1, replica_groups=mesh['half'=2,'ring'=16,'lat'=16] {'ring'}, dimensions={0} | all-to-all | bytes 262144 | tf_op jit(solution)/shard_map/all_to_all | solution.py:287
  55.3 0.6 spread.1
  55.9 6.6 %all-to-all-start.2 = ((f32[16,1,128]{2,1,0:T(1,128)}), f32[16,1,128]{2,1,0:T(1,128)S(1)}, u32[]{:S(2)}, u32[]{:S(2)}) async-start(f32[16,1,128]{2,1,0:T(1,128)} %spread.1), calls=%async_computation.2 | async-start | bytes 16384 | tf_op jit(solution)/shard_map/all_to_all | solution.py:288
  62.5 1.6 %finish.1 = f32[8,128,256]{2,1,0:T(8,128)} custom-call(f32[2048,128]{1,0:T(8,128)S(1)} %get-tuple-element.6.source_t, f32[2048,128]{1,0:T(8,128)S(1)} %get-tuple-element.7.courant_t, f32[16,8,128]{2,1,0:T(8,128)S(1)} %get-tuple-element.8.entries, f32[256,128]{1,0:T(8,128)S(1)} %bitcast.9), custom_call_target="tpu_custom_call" | custom-call | tf_op jit(solution)/shard_map/finish/pallas_call | solution.py:239
  64.1 5.2 %all-to-all-done.2.sums = f32[16,1,128]{2,1,0:T(1,128)S(1)} async-done(((f32[16,1,128]{2,1,0:T(1,128)}), f32[16,1,128]{2,1,0:T(1,128)S(1)}, u32[]{:S(2)}, u32[]{:S(2)}) %all-to-all-start.2) | async-done | bytes 8224 | tf_op jit(solution)/shard_map/all_to_all | solution.py:288
  69.3 0.6 mean.1
  (2 shorter events, 0.0 us)
Async XLA Ops:
  22.7 18.0 %collective-permute-start = (f32[16,16,128]{2,1,0:T(8,128)S(1)}, f32[16,16,128]{2,1,0:T(8,128)S(1)}, u32[]{:S(2)}, u32[]{:S(2)}) collective-permute-start(f32[16,16,128]{2,1,0:T(8,128)S(1)} %slice.8), channel_id=1, source_target_pairs={{0,256},{1,1},{2,2},{3,3},{4,4},{5,5},{6,6},{7,7},{8,8},{9,9},{10,... | collective-permute-start | bytes 393224 | tf_op jit(solution)/shard_map/ppermute | solution.py:278
  32.4 8.3 %collective-permute-start.1 = (f32[16,128]{1,0:T(8,128)S(1)}, f32[16,128]{1,0:T(8,128)S(1)}, u32[]{:S(2)}, u32[]{:S(2)}) collective-permute-start(f32[16,128]{1,0:T(8,128)S(1)} %bitcast.11), channel_id=1, source_target_pairs={{0,256},{256,0},{1,257},{257,1},{2,258},{258,2},{3,259},{259,3},{4... | collective-permute-start | bytes 24584 | tf_op jit(solution)/shard_map/ppermute | solution.py:279
  55.9 13.4 %all-to-all-start.2 = ((f32[16,1,128]{2,1,0:T(1,128)}), f32[16,1,128]{2,1,0:T(1,128)S(1)}, u32[]{:S(2)}, u32[]{:S(2)}) async-start(f32[16,1,128]{2,1,0:T(1,128)} %spread.1), calls=%async_computation.2 | async-start | bytes 16384 | tf_op jit(solution)/shard_map/all_to_all | solution.py:288

commit v4 on v3

--- a/solution.py
+++ b/solution.py
@@ -8,8 +8,8 @@
 HALVES, RING, LEVELS, ROWS, CELLS, SLAB = 2, 16, 8, 128, 256, 8
 SEGMENTS = 8
 STEPS = CELLS // SEGMENTS
-SENT = 24
-BACK = 16
+SENT = 17
+BACK = 10
 
 VMEM = pl.BlockSpec(memory_space=pltpu.VMEM)
 SMEM = pl.BlockSpec(memory_space=pltpu.SMEM)
@@ -66,15 +66,13 @@
         g, o = g * growth[k], growth[k] * o + offset[k]
     low = lanes((LEVELS, ROWS)) < 64
     maps = (jnp.where(low, g, pltpu.roll(o, 64, 1)), jnp.where(low, pltpu.roll(g, 64, 1), o))
-    zeros = jnp.zeros((SENT - 16, 128), jnp.float32)
     for r in range(SLAB):
         for a in range(4):
             x = slab[a, pl.ds(r, LEVELS, stride=SLAB), :]
-            sent[2 * r, pl.ds(4 * a, 4), :] = x[:4]
-            sent[2 * r + 1, pl.ds(4 * a, 4), :] = x[4:]
+            sent[pl.ds(SENT * 2 * r + 4 * a, 4), :] = x[:4]
+            sent[pl.ds(SENT * (2 * r + 1) + 4 * a, 4), :] = x[4:]
         for parity in range(2):
-            sent[2 * r + parity, pl.ds(16, SENT - 16), :] = zeros
-            sent[2 * r + parity, pl.ds(16, 1), :] = maps[parity][r : r + 1]
+            sent[pl.ds(SENT * (2 * r + parity) + 16, 1), :] = maps[parity][r : r + 1]
 
 
 def pack(tracer, courant):
@@ -82,7 +80,7 @@
     return pl.pallas_call(
         pack_kernel,
         out_shape=(
-            pltpu.VMEM((RING, SENT, 128), f32),
+            pltpu.VMEM((RING * SENT, 128), f32),
             pltpu.VMEM((CELLS * LEVELS, ROWS), f32),
             pltpu.VMEM((CELLS * LEVELS, ROWS), f32),
             pltpu.VMEM((2 * SEGMENTS, LEVELS, ROWS), f32),
@@ -99,13 +97,13 @@
     )(tracer, courant)
 
 
-def solve_kernel(hops, area, own, far_slab, far_maps, back, source, courant, source_t, courant_t):
+def solve_kernel(hops, area, own, far, far_maps, back, source, courant, source_t, courant_t):
     half = lax.axis_index("half")
     ring = lax.axis_index("ring")
     polar, start = polar_start()
     row, parity = ring // 2, ring % 2
     for d in range(HALVES * RING):
-        ref, base = (own, d * SENT) if d < RING else (far_slab, (d - RING) * 16)
+        ref, base = (own if d < RING else far), (d % RING) * SENT
         for side in range(2):
             to = pl.ds(side * 128, 128)
             source[pl.ds(4 * d, 4), to] = ref[pl.ds(base + 4 * side, 4), :]
@@ -150,7 +148,8 @@
             source_t[at, :] = u
             flux[k] = c * u
     source[...] = source_t[...].T
-    x = jnp.concatenate([own[pl.ds(16, RING, stride=SENT), :], far_maps[...]], 0)
+    at = pl.ds(16, RING, stride=SENT)
+    x = jnp.concatenate([own[at, :], jnp.where(polar, far[at, :], far_maps[...])], 0)
     low = lanes(x.shape) < 64
     turned = pltpu.roll(x, 64, 1)
     rest_g = jnp.where(low, x, turned)
@@ -172,25 +171,23 @@
     sums = sums + jnp.where((lane >= 4 * parity) & (lane < 4 * parity + 4), loops, 0.0)
     total = jnp.sum(areas, axis=1, keepdims=True)
     sums = jnp.where(lane == 8, jnp.where(ring == 0, total, 0.0), sums)
-    zeros = jnp.zeros((BACK - 8, 128), jnp.float32)
     for d in range(RING):
         for side in range(2):
-            back[d, pl.ds(4 * side, 4), :] = source[pl.ds(4 * d, 4), pl.ds(side * 128, 128)]
-        back[d, pl.ds(8, BACK - 8), :] = zeros
-        back[d, pl.ds(8, 1), :] = rest[d : d + 1]
-        back[d, pl.ds(9, 1), :] = sums
-
-
-def solve(hops, area, own, far_slab, far_maps):
+            back[pl.ds(BACK * d + 4 * side, 4), :] = source[pl.ds(4 * d, 4), pl.ds(side * 128, 128)]
+        back[pl.ds(BACK * d + 8, 1), :] = rest[d : d + 1]
+        back[pl.ds(BACK * d + 9, 1), :] = sums
+
+
+def solve(hops, area, own, far, far_maps):
     f32 = jnp.float32
     return pl.pallas_call(
         solve_kernel,
-        out_shape=pltpu.VMEM((RING, BACK, 128), f32),
+        out_shape=pltpu.VMEM((RING * BACK, 128), f32),
         in_specs=[SMEM] + [VMEM] * 4,
         out_specs=VMEM,
         scratch_shapes=[pltpu.VMEM((ROWS, CELLS), f32)] * 2 + [pltpu.VMEM((CELLS, ROWS), f32)] * 2,
         name="solve",
-    )(hops, area, *in_vmem(own, far_slab, far_maps))
+    )(hops, area, *in_vmem(own, far, far_maps))
 
 
 def spread_kernel(got, sums):
@@ -264,27 +261,29 @@
     )(*in_vmem(sums))
 
 
+def exchange(rows):
+    blocks = rows.reshape(RING, -1, 1, 128)
+    return lax.all_to_all(blocks, "ring", 0, 0, tiled=True).reshape(rows.shape)
+
+
 def body(tracer, courant, hop_counts, row_area):
     lats = lax.axis_size("lat")
 
-    def across(i):
-        h, rest = divmod(i, RING * lats)
-        moved = rest % lats in (0, lats - 1)
-        return (i, (1 - h) * RING * lats + rest if moved else i)
+    def across(polar):
+        half = RING * lats
+        pairs = []
+        for i in range(HALVES * half):
+            moved = (i % lats in (0, lats - 1)) == polar
+            pairs.append((i, (i + half) % (HALVES * half) if moved else i))
+        return pairs
 
     sent, source_t, courant_t, entries = pack(tracer, courant)
-    got = lax.all_to_all(sent, "ring", 0, 0, tiled=True)
+    got = exchange(sent)
     every = ("half", "ring", "lat")
-    far_slab = lax.ppermute(got[:, :16], every, [across(i) for i in range(HALVES * RING * lats)])
-    far_maps = lax.ppermute(got[:, 16], "half", [(0, 1), (1, 0)])
-    back = solve(
-        hop_counts,
-        row_area.reshape(1, ROWS),
-        got.reshape(RING * SENT, 128),
-        far_slab.reshape(RING * 16, 128),
-        far_maps,
-    )
-    back = lax.all_to_all(back, "ring", 0, 0, tiled=True).reshape(RING * BACK, 128)
+    far = lax.ppermute(got, every, across(True))
+    far_maps = lax.ppermute(lax.slice(got, (16, 0), (RING * SENT, 128), (SENT, 1)), every, across(False))
+    back = solve(hop_counts, row_area.reshape(1, ROWS), got, far, far_maps)
+    back = exchange(back)
     sums = lax.all_to_all(spread(back, lats), "lat", 0, 0, tiled=True)
     return finish(source_t, courant_t, entries, back), mean(sums)
 

time: 70.2 us -> 62.8 us (0.89)
  blocking collectives: 32.6 us -> 29.7 us
  waiting for transfers between devices: 11.6 us -> 8.75 us
  starting transfers between devices: 18.2 us -> 16.6 us
    all_to_all x2, blocking collectives: 32.6 us -> 29.7 us  [exchange(): return lax.all_to_all(blocks, 'ring', 0, 0, tiled=True).reshape(rows.shape)]
    ppermute x2, waiting for transfers between devices: 6.38 us -> 3.51 us  [the longest x1 3.5 us: body(): far = lax.ppermute(got, every, across(True))]
    ppermute x2, starting transfers between devices: 11.6 us -> 10.2 us  [the longest x1 9.49 us: body(): far = lax.ppermute(got, every, across(True))]
where the time goes in v4:
time: 62.8 us; the launch traced here: 62.5 us
  blocking collectives  29.7 us (47%)
  starting transfers between devices  16.6 us (26%)
  waiting for transfers between devices  8.75 us (14%)
  Pallas kernels  6.81 us (11%)
  between operations  0.68 us (1%)
    all_to_all x2, blocking collectives, exchange(): return lax.all_to_all(blocks, 'ring', 0, 0, tiled=True).reshape(rows.shape)  29.7 us
    ppermute x1, starting transfers between devices, body(): far = lax.ppermute(got, every, across(True))  9.49 us
    all_to_all x1, starting transfers between devices, body(): sums = lax.all_to_all(spread(back, lats), 'lat', 0, 0, tiled=True)  6.49 us
    all_to_all x1, waiting for transfers between devices, body(): sums = lax.all_to_all(spread(back, lats), 'lat', 0, 0, tiled=True)  5.24 us
    ppermute x1, waiting for transfers between devices, body(): far = lax.ppermute(got, every, across(True))  3.5 us
    pallas_call x1, Pallas kernels, pack(): pl.pallas_call(pack_kernel, out_shape=(pltpu.VMEM((RING * SENT, 128), f32...  2.48 us
    pallas_call x1, Pallas kernels, solve(): pl.pallas_call(solve_kernel, out_shape=pltpu.VMEM((RING * BACK, 128), f32...  1.55 us
    pallas_call x1, Pallas kernels, finish(): pl.pallas_call(finish_kernel, out_shape=jax.ShapeDtypeStruct((LEVELS, ROW...  1.55 us
  transfers between devices with their start and end apart: 3, of which 2 were waited for; matrix products, arithmetic and copies ran while one was open for 0% of the time, Pallas kernels for 2%

profile of v4, /device:TPU:1, one launch (start us, length us, event | category | flops | bytes accessed | tf_op | source)
XLA Modules:
  0.0 62.5 jit_solution(1281082209528702825)
XLA Ops:
  0.6 2.5 %pack.1 = (f32[272,128]{1,0:T(8,128)S(1)}, f32[2048,128]{1,0:T(8,128)S(1)}, f32[2048,128]{1,0:T(8,128)S(1)}, f32[16,8,128]{2,1,0:T(8,128)S(1)}) custom-call(f32[8,128,256]{2,1,0:T(8,128)} %tracer.1, f32[8,128,256]{2,1,0:T(8,128)} %courant.1), custom_call_target="tpu_custom_call" | custom-call | tf_op jit(solution)/shard_map/pack/pallas_call | solution.py:80
  3.1 18.6 %all_to_all.15 = f32[16,17,1,128]{3,2,1,0:T(1,128)S(1)} all-to-all(f32[16,17,1,128]{3,2,1,0:T(1,128)S(1)} %bitcast.11), channel_id=1, replica_groups=mesh['half'=2,'ring'=16,'lat'=16] {'ring'}, dimensions={0} | all-to-all | bytes 278528 | tf_op jit(solution)/shard_map/all_to_all | solution.py:266
  21.7 9.5 %collective-permute-start = (f32[272,128]{1,0:T(8,128)S(1)}, f32[272,128]{1,0:T(8,128)S(1)}, u32[]{:S(2)}, u32[]{:S(2)}) collective-permute-start(f32[272,128]{1,0:T(8,128)S(1)} %bitcast.7), channel_id=1, source_target_pairs={{0,256},{1,1},{2,2},{3,3},{4,4},{5,5},{6,6},{7,7},{8,8},{9,9},{10,... | collective-permute-start | bytes 417800 | tf_op jit(solution)/shard_map/ppermute | solution.py:283
  31.2 0.7 %collective-permute-start.1 = (f32[16,128]{1,0:T(8,128)S(1)}, f32[16,128]{1,0:T(8,128)S(1)}, u32[]{:S(2)}, u32[]{:S(2)}) collective-permute-start(f32[16,128]{1,0:T(8,128)S(1)} %slice.3), channel_id=1, source_target_pairs={{0,0},{1,257},{2,258},{3,259},{4,260},{5,261},{6,262},{7,263},{8,2... | collective-permute-start | bytes 24584 | tf_op jit(solution)/shard_map/ppermute | solution.py:284
  31.9 0.0 collective-permute-done.1.far_maps
  31.9 3.5 %collective-permute-done.far = f32[272,128]{1,0:T(8,128)S(1)} collective-permute-done((f32[272,128]{1,0:T(8,128)S(1)}, f32[272,128]{1,0:T(8,128)S(1)}, u32[]{:S(2)}, u32[]{:S(2)}) %collective-permute-start) | collective-permute-done | bytes 139296 | tf_op jit(solution)/shard_map/ppermute | solution.py:283
  35.4 1.6 %solve.1 = f32[160,128]{1,0:T(8,128)S(1)} custom-call(s32[128]{0:T(128)} %hops.1, f32[1,128]{1,0:T(1,128)} %bitcast.12, f32[272,128]{1,0:T(8,128)S(1)} %bitcast.9, f32[272,128]{1,0:T(8,128)S(1)} %collective-permute-done.far, f32[16,128]{1,0:T(8,128)S(1)} %collective-permute-done.1.far_maps), custom_call_target="tpu_custom_call" | custom-call | tf_op jit(solution)/shard_map/solve/pallas_call | solution.py:183
  37.0 11.1 %all_to_all.16 = f32[16,10,1,128]{3,2,1,0:T(1,128)S(1)} all-to-all(f32[16,10,1,128]{3,2,1,0:T(1,128)S(1)} %bitcast.10), channel_id=1, replica_groups=mesh['half'=2,'ring'=16,'lat'=16] {'ring'}, dimensions={0} | all-to-all | bytes 163840 | tf_op jit(solution)/shard_map/all_to_all | solution.py:266
  48.0 0.6 spread.1
  48.6 6.5 %all-to-all-start.2 = ((f32[16,1,128]{2,1,0:T(1,128)}), f32[16,1,128]{2,1,0:T(1,128)S(1)}, u32[]{:S(2)}, u32[]{:S(2)}) async-start(f32[16,1,128]{2,1,0:T(1,128)} %spread.1), calls=%async_computation.2 | async-start | bytes 16384 | tf_op jit(solution)/shard_map/all_to_all | solution.py:287
  55.1 1.5 %finish.1 = f32[8,128,256]{2,1,0:T(8,128)} custom-call(f32[2048,128]{1,0:T(8,128)S(1)} %get-tuple-element.6.source_t, f32[2048,128]{1,0:T(8,128)S(1)} %get-tuple-element.7.courant_t, f32[16,8,128]{2,1,0:T(8,128)S(1)} %get-tuple-element.8.entries, f32[160,128]{1,0:T(8,128)S(1)} %bitcast.6), custom_call_target="tpu_custom_call" | custom-call | tf_op jit(solution)/shard_map/finish/pallas_call | solution.py:236
  56.7 5.2 %all-to-all-done.2.sums = f32[16,1,128]{2,1,0:T(1,128)S(1)} async-done(((f32[16,1,128]{2,1,0:T(1,128)}), f32[16,1,128]{2,1,0:T(1,128)S(1)}, u32[]{:S(2)}, u32[]{:S(2)}) %all-to-all-start.2) | async-done | bytes 8224 | tf_op jit(solution)/shard_map/all_to_all | solution.py:287
  61.9 0.6 mean.1
  (1 shorter events, 0.0 us)
Async XLA Ops:
  21.7 13.7 %collective-permute-start = (f32[272,128]{1,0:T(8,128)S(1)}, f32[272,128]{1,0:T(8,128)S(1)}, u32[]{:S(2)}, u32[]{:S(2)}) collective-permute-start(f32[272,128]{1,0:T(8,128)S(1)} %bitcast.7), channel_id=1, source_target_pairs={{0,256},{1,1},{2,2},{3,3},{4,4},{5,5},{6,6},{7,7},{8,8},{9,9},{10,... | collective-permute-start | bytes 417800 | tf_op jit(solution)/shard_map/ppermute | solution.py:283
  31.2 0.7 %collective-permute-start.1 = (f32[16,128]{1,0:T(8,128)S(1)}, f32[16,128]{1,0:T(8,128)S(1)}, u32[]{:S(2)}, u32[]{:S(2)}) collective-permute-start(f32[16,128]{1,0:T(8,128)S(1)} %slice.3), channel_id=1, source_target_pairs={{0,0},{1,257},{2,258},{3,259},{4,260},{5,261},{6,262},{7,263},{8,2... | collective-permute-start | bytes 24584 | tf_op jit(solution)/shard_map/ppermute | solution.py:284
  48.6 13.3 %all-to-all-start.2 = ((f32[16,1,128]{2,1,0:T(1,128)}), f32[16,1,128]{2,1,0:T(1,128)S(1)}, u32[]{:S(2)}, u32[]{:S(2)}) async-start(f32[16,1,128]{2,1,0:T(1,128)} %spread.1), calls=%async_computation.2 | async-start | bytes 16384 | tf_op jit(solution)/shard_map/all_to_all | solution.py:287

commit v5 on v4

--- a/solution.py
+++ b/solution.py
@@ -6,13 +6,13 @@
 from jax.sharding import Mesh, PartitionSpec as P
 
 HALVES, RING, LEVELS, ROWS, CELLS, SLAB = 2, 16, 8, 128, 256, 8
+STOPS = 7
 SEGMENTS = 8
 STEPS = CELLS // SEGMENTS
 SENT = 17
 BACK = 10
 
 VMEM = pl.BlockSpec(memory_space=pltpu.VMEM)
-SMEM = pl.BlockSpec(memory_space=pltpu.SMEM)
 
 
 def lanes(shape):
@@ -29,7 +29,13 @@
     return [pltpu.with_memory_space_constraint(x, pltpu.VMEM) for x in arrays]
 
 
-def pack_kernel(tracer, courant, sent, source_t, courant_t, entries, source, factor, slab, sems):
+def pack_kernel(
+    tracer, courant, hops, area, sent, source_t, courant_t, entries, hops_out, area_out, source, factor, slab, sems
+):
+    rows = (
+        pltpu.make_async_copy(hops, hops_out, sems.at[2, 0]),
+        pltpu.make_async_copy(area, area_out, sems.at[2, 1]),
+    )
     copies = [
         (
             pltpu.make_async_copy(tracer.at[l], source.at[l], sems.at[0, l]),
@@ -37,7 +43,7 @@
         )
         for l in range(LEVELS)
     ]
-    for pair in copies:
+    for pair in (*copies, rows):
         for copy in pair:
             copy.start()
     _, start = polar_start()
@@ -73,9 +79,11 @@
             sent[pl.ds(SENT * (2 * r + 1) + 4 * a, 4), :] = x[4:]
         for parity in range(2):
             sent[pl.ds(SENT * (2 * r + parity) + 16, 1), :] = maps[parity][r : r + 1]
-
-
-def pack(tracer, courant):
+    for copy in rows:
+        copy.wait()
+
+
+def pack(tracer, courant, hops, area):
     f32 = jnp.float32
     return pl.pallas_call(
         pack_kernel,
@@ -84,17 +92,19 @@
             pltpu.VMEM((CELLS * LEVELS, ROWS), f32),
             pltpu.VMEM((CELLS * LEVELS, ROWS), f32),
             pltpu.VMEM((2 * SEGMENTS, LEVELS, ROWS), f32),
+            pltpu.VMEM((1, ROWS), jnp.int32),
+            pltpu.VMEM((1, ROWS), f32),
         ),
-        in_specs=[pl.BlockSpec(memory_space=pl.ANY)] * 2,
-        out_specs=(VMEM,) * 4,
+        in_specs=[pl.BlockSpec(memory_space=pl.ANY)] * 4,
+        out_specs=(VMEM,) * 6,
         scratch_shapes=[
             pltpu.VMEM((LEVELS, ROWS, CELLS), f32),
             pltpu.VMEM((LEVELS, ROWS, CELLS), f32),
             pltpu.VMEM((4, LEVELS * SLAB, 128), f32),
-            pltpu.SemaphoreType.DMA((2, LEVELS)),
+            pltpu.SemaphoreType.DMA((3, LEVELS)),
         ],
         name="pack",
-    )(tracer, courant)
+    )(tracer, courant, hops, area)
 
 
 def solve_kernel(hops, area, own, far, far_maps, back, source, courant, source_t, courant_t):
@@ -108,7 +118,13 @@
             to = pl.ds(side * 128, 128)
             source[pl.ds(4 * d, 4), to] = ref[pl.ds(base + 4 * side, 4), :]
             courant[pl.ds(4 * d, 4), to] = ref[pl.ds(base + 8 + 4 * side, 4), :]
-    source_t[...] = pltpu.roll(source[...].T, 4 * hops[start + row], 1)
+    lane = lanes((1, 128))
+    slab_row = lane == start + row
+    hop = jnp.sum(jnp.where(slab_row, hops[...].astype(jnp.float32), 0.0), axis=1, keepdims=True).astype(jnp.int32)
+    shifted = source[...].T
+    for bit in range(STOPS.bit_length()):
+        shifted = jnp.where((hop >> bit) % 2 == 1, pltpu.roll(shifted, 4 << bit, 1), shifted)
+    source_t[...] = shifted
     courant_t[...] = courant[...].T
     parts = range(CELLS // 64)
     growth = [jnp.ones((8, ROWS), jnp.float32) for k in parts]
@@ -159,13 +175,12 @@
         rest_g = rest_g * pltpu.roll(rest_g, stride, 0)
     rest = pltpu.roll(rest_o / (1.0 - rest_g), 1, 0)
     wrap = jnp.where(half == 0, rest[:1], rest[RING : RING + 1])
-    lane = lanes((1, 128))
     areas = area[...]
     mine = lane // 64 == parity
     in_slab = polar & (lane >= start) & (lane < start + SLAB)
     weighted = jnp.where(mine & ~in_slab, areas, 0.0) * wrap
     weighted = jnp.sum(weighted, axis=1, keepdims=True)
-    slab_area = jnp.sum(jnp.where(polar & (lane == start + row), areas, 0.0), axis=1, keepdims=True)
+    slab_area = jnp.sum(jnp.where(polar & slab_row, areas, 0.0), axis=1, keepdims=True)
     loops = pltpu.roll(inflow, (4 * parity + 128 - 64 * half) % 128, 1) * slab_area
     sums = jnp.where(lane == row, weighted, 0.0)
     sums = sums + jnp.where((lane >= 4 * parity) & (lane < 4 * parity + 4), loops, 0.0)
@@ -183,11 +198,11 @@
     return pl.pallas_call(
         solve_kernel,
         out_shape=pltpu.VMEM((RING * BACK, 128), f32),
-        in_specs=[SMEM] + [VMEM] * 4,
+        in_specs=[VMEM] * 5,
         out_specs=VMEM,
         scratch_shapes=[pltpu.VMEM((ROWS, CELLS), f32)] * 2 + [pltpu.VMEM((CELLS, ROWS), f32)] * 2,
         name="solve",
-    )(hops, area, *in_vmem(own, far, far_maps))
+    )(*in_vmem(hops, area, own, far, far_maps))
 
 
 def spread_kernel(got, sums):
@@ -199,14 +214,14 @@
 def spread(got, lats):
     return pl.pallas_call(
         spread_kernel,
-        out_shape=jax.ShapeDtypeStruct((lats, 1, 128), jnp.float32),
+        out_shape=pltpu.VMEM((lats, 1, 128), jnp.float32),
         in_specs=[VMEM],
         out_specs=VMEM,
         name="spread",
     )(*in_vmem(got))
 
 
-def finish_kernel(source_t, courant_t, entries, got, updated, updated_t):
+def finish_kernel(source_t, courant_t, entries, got, sums, updated, mean, updated_t, level, sems):
     low = lanes((LEVELS, ROWS)) < 64
     even = got[pl.ds(8, LEVELS, stride=2 * BACK), :]
     odd = got[pl.ds(8 + BACK, LEVELS, stride=2 * BACK), :]
@@ -219,46 +234,44 @@
             u = (source_t[at, :] + flux[k]) * (1.0 / (1.0 + c))
             updated_t[at, :] = u
             flux[k] = c * u
+    polar, start = polar_start()
+    rows = pl.ds(start, SLAB)
+    copies = []
     for l in range(LEVELS):
-        updated[l] = updated_t[pl.ds(l, CELLS, stride=LEVELS), :].T
-    polar, start = polar_start()
-
-    @pl.when(polar)
-    def _():
-        rows = pl.ds(start, SLAB)
-        for l in range(LEVELS):
-            for side in range(2):
-                at = (l // 4) * BACK + 4 * side + l % 4
-                updated[l, rows, pl.ds(side * 128, 128)] = got[pl.ds(at, SLAB, stride=2 * BACK), :]
-
-
-def finish(source_t, courant_t, entries, got):
-    return pl.pallas_call(
-        finish_kernel,
-        out_shape=jax.ShapeDtypeStruct((LEVELS, ROWS, CELLS), jnp.float32),
-        in_specs=[VMEM] * 4,
-        out_specs=VMEM,
-        scratch_shapes=[pltpu.VMEM((CELLS * LEVELS, ROWS), jnp.float32)],
-        name="finish",
-    )(*in_vmem(source_t, courant_t, entries, got))
-
-
-def mean_kernel(sums, mean):
+        level[l] = updated_t[pl.ds(l, CELLS, stride=LEVELS), :].T
+        for side in range(2):
+            to = pl.ds(side * 128, 128)
+            at = (l // 4) * BACK + 4 * side + l % 4
+            solved = got[pl.ds(at, SLAB, stride=2 * BACK), :]
+            level[l, rows, to] = jnp.where(polar, solved, level[l, rows, to])
+        copies.append(pltpu.make_async_copy(level.at[l], updated.at[l], sems.at[l]))
+        copies[l].start()
     total = sums[0]
     for i in range(1, sums.shape[0]):
         total = total + sums[i]
     area = jnp.sum(jnp.where(lanes((1, 128)) == 8, total, 0.0), axis=1, keepdims=True)
     mean[...] = (total / area)[0, :LEVELS]
-
-
-def mean(sums):
+    for copy in copies:
+        copy.wait()
+
+
+def finish(source_t, courant_t, entries, got, sums):
+    f32 = jnp.float32
     return pl.pallas_call(
-        mean_kernel,
-        out_shape=jax.ShapeDtypeStruct((LEVELS,), jnp.float32),
-        in_specs=[VMEM],
-        out_specs=VMEM,
-        name="mean",
-    )(*in_vmem(sums))
+        finish_kernel,
+        out_shape=(
+            jax.ShapeDtypeStruct((LEVELS, ROWS, CELLS), f32),
+            jax.ShapeDtypeStruct((LEVELS,), f32),
+        ),
+        in_specs=[VMEM] * 5,
+        out_specs=(pl.BlockSpec(memory_space=pl.ANY), VMEM),
+        scratch_shapes=[
+            pltpu.VMEM((CELLS * LEVELS, ROWS), f32),
+            pltpu.VMEM((LEVELS, ROWS, CELLS), f32),
+            pltpu.SemaphoreType.DMA((LEVELS,)),
+        ],
+        name="finish",
+    )(*in_vmem(source_t, courant_t, entries, got, sums))
 
 
 def exchange(rows):
@@ -277,15 +290,16 @@
             pairs.append((i, (i + half) % (HALVES * half) if moved else i))
         return pairs
 
-    sent, source_t, courant_t, entries = pack(tracer, courant)
+    hops, area = hop_counts.reshape(1, ROWS), row_area.reshape(1, ROWS)
+    sent, source_t, courant_t, entries, hops, area = pack(tracer, courant, hops, area)
     got = exchange(sent)
     every = ("half", "ring", "lat")
     far = lax.ppermute(got, every, across(True))
     far_maps = lax.ppermute(lax.slice(got, (16, 0), (RING * SENT, 128), (SENT, 1)), every, across(False))
-    back = solve(hop_counts, row_area.reshape(1, ROWS), got, far, far_maps)
+    back = solve(hops, area, got, far, far_maps)
     back = exchange(back)
     sums = lax.all_to_all(spread(back, lats), "lat", 0, 0, tiled=True)
-    return finish(source_t, courant_t, entries, back), mean(sums)
+    return finish(source_t, courant_t, entries, back, sums)
 
 
 def solution(mesh):

time: 62.8 us -> 62.8 us (level)
  blocking collectives: 29.7 us -> 42.7 us
  starting transfers between devices: 16.6 us -> 10.2 us
  waiting for transfers between devices: 8.75 us -> 3.51 us
  Pallas kernels: 6.81 us -> 5.46 us
    all_to_all x0 -> x1, blocking collectives: none -> 13.1 us  [body(): sums = lax.all_to_all(spread(back, lats), 'lat', 0, 0, tiled=True)]
    all_to_all x1 -> x0, starting transfers between devices: 6.49 us -> none  [body(): sums = lax.all_to_all(spread(back, lats), 'lat', 0, 0, tiled=True)]
    all_to_all x1 -> x0, waiting for transfers between devices: 5.24 us -> none  [body(): sums = lax.all_to_all(spread(back, lats), 'lat', 0, 0, tiled=True)]
    pallas_call x3 -> x2, Pallas kernels: 2.77 us -> 1.89 us  [the longest x1 1.88 us: finish(): pl.pallas_call(finish_kernel, out_shape=(jax.ShapeDtypeStruct((LEVELS, RO...]
  transfers between devices with their start and end apart: 3 -> 2, of which waited for: 2 -> 1; matrix products, arithmetic and copies ran while one was open for 0% -> 0% of each run, Pallas kernels for 2% -> 0%
where the time goes in v5:
time: 62.8 us; the launch traced here: 62.5 us
  blocking collectives  42.7 us (68%)
  starting transfers between devices  10.2 us (16%)
  Pallas kernels  5.46 us (9%)
  waiting for transfers between devices  3.51 us (6%)
  between operations  0.67 us (1%)
    all_to_all x2, blocking collectives, exchange(): return lax.all_to_all(blocks, 'ring', 0, 0, tiled=True).reshape(rows.shape)  29.7 us
    all_to_all x1, blocking collectives, body(): sums = lax.all_to_all(spread(back, lats), 'lat', 0, 0, tiled=True)  13.1 us
    ppermute x1, starting transfers between devices, body(): far = lax.ppermute(got, every, across(True))  9.49 us
    ppermute x1, waiting for transfers between devices, body(): far = lax.ppermute(got, every, across(True))  3.5 us
    pallas_call x1, Pallas kernels, pack(): pl.pallas_call(pack_kernel, out_shape=(pltpu.VMEM((RING * SENT, 128), f32...  2.56 us
    pallas_call x1, Pallas kernels, finish(): pl.pallas_call(finish_kernel, out_shape=(jax.ShapeDtypeStruct((LEVELS, RO...  1.88 us
  transfers between devices with their start and end apart: 2, of which 1 were waited for; matrix products, arithmetic and copies ran while one was open for 0% of the time, Pallas kernels for 0%

profile of v5, /device:TPU:1, one launch (start us, length us, event | category | flops | bytes accessed | tf_op | source)
XLA Modules:
  0.0 62.5 jit_solution(9384523831453408829)
XLA Ops:
  0.6 2.6 %pack.1 = (f32[272,128]{1,0:T(8,128)S(1)}, f32[2048,128]{1,0:T(8,128)S(1)}, f32[2048,128]{1,0:T(8,128)S(1)}, f32[16,8,128]{2,1,0:T(8,128)S(1)}, s32[1,128]{1,0:T(1,128)S(1)}, /*index=5*/f32[1,128]{1,0:T(1,128)S(1)}) custom-call(f32[8,128,256]{2,1,0:T(8,128)} %tracer.1, f32[8,128,256]{2,1,0:T(8,128)} %courant.1, s32[1,128]{1,0:T(1,128)} %bitcast.13, ...), custom_call_target="tpu_custom_call" | custom-call | tf_op jit(solution)/shard_map/pack/pallas_call | solution.py:88
  3.2 18.6 %all_to_all.15 = f32[16,17,1,128]{3,2,1,0:T(1,128)S(1)} all-to-all(f32[16,17,1,128]{3,2,1,0:T(1,128)S(1)} %bitcast.12), channel_id=1, replica_groups=mesh['half'=2,'ring'=16,'lat'=16] {'ring'}, dimensions={0} | all-to-all | bytes 278528 | tf_op jit(solution)/shard_map/all_to_all | solution.py:279
  21.8 9.5 %collective-permute-start = (f32[272,128]{1,0:T(8,128)S(1)}, f32[272,128]{1,0:T(8,128)S(1)}, u32[]{:S(2)}, u32[]{:S(2)}) collective-permute-start(f32[272,128]{1,0:T(8,128)S(1)} %bitcast.8), channel_id=1, source_target_pairs={{0,256},{1,1},{2,2},{3,3},{4,4},{5,5},{6,6},{7,7},{8,8},{9,9},{10,... | collective-permute-start | bytes 417800 | tf_op jit(solution)/shard_map/ppermute | solution.py:297
  31.3 0.7 %collective-permute-start.1 = (f32[16,128]{1,0:T(8,128)S(1)}, f32[16,128]{1,0:T(8,128)S(1)}, u32[]{:S(2)}, u32[]{:S(2)}) collective-permute-start(f32[16,128]{1,0:T(8,128)S(1)} %slice.3), channel_id=1, source_target_pairs={{0,0},{1,257},{2,258},{3,259},{4,260},{5,261},{6,262},{7,263},{8,2... | collective-permute-start | bytes 24584 | tf_op jit(solution)/shard_map/ppermute | solution.py:298
  32.0 0.0 collective-permute-done.1.far_maps
  32.0 3.5 %collective-permute-done.far = f32[272,128]{1,0:T(8,128)S(1)} collective-permute-done((f32[272,128]{1,0:T(8,128)S(1)}, f32[272,128]{1,0:T(8,128)S(1)}, u32[]{:S(2)}, u32[]{:S(2)}) %collective-permute-start) | collective-permute-done | bytes 139296 | tf_op jit(solution)/shard_map/ppermute | solution.py:297
  35.5 1.0 %solve.1 = f32[160,128]{1,0:T(8,128)S(1)} custom-call(s32[1,128]{1,0:T(1,128)S(1)} %get-tuple-element.11.hops, f32[1,128]{1,0:T(1,128)S(1)} %get-tuple-element.12.area, f32[272,128]{1,0:T(8,128)S(1)} %bitcast.10, f32[272,128]{1,0:T(8,128)S(1)} %collective-permute-done.far, f32[16,128]{1,0:T(8,128)S(1)} %collective-permute-done.1.far_maps), custom_call_target="tpu_custom_call" | custom-call | tf_op jit(solution)/shard_map/solve/pallas_call | solution.py:198
  36.5 11.1 %all_to_all.16 = f32[16,10,1,128]{3,2,1,0:T(1,128)S(1)} all-to-all(f32[16,10,1,128]{3,2,1,0:T(1,128)S(1)} %bitcast.11), channel_id=1, replica_groups=mesh['half'=2,'ring'=16,'lat'=16] {'ring'}, dimensions={0} | all-to-all | bytes 163840 | tf_op jit(solution)/shard_map/all_to_all | solution.py:279
  47.6 13.1 %all_to_all.17.sums = f32[16,1,128]{2,1,0:T(1,128)S(1)} all-to-all(f32[16,1,128]{2,1,0:T(1,128)S(1)} %spread.1), channel_id=1, replica_groups=mesh['half'=2,'ring'=16,'lat'=16] {'lat'}, dimensions={0} | all-to-all | bytes 16384 | tf_op jit(solution)/shard_map/all_to_all | solution.py:301
  60.7 1.9 %finish.1 = (f32[8,128,256]{2,1,0:T(8,128)}, f32[8]{0:T(128)}) custom-call(f32[2048,128]{1,0:T(8,128)S(1)} %get-tuple-element.8.source_t, f32[2048,128]{1,0:T(8,128)S(1)} %get-tuple-element.9.courant_t, f32[16,8,128]{2,1,0:T(8,128)S(1)} %get-tuple-element.10.entries, f32[160,128]{1,0:T(8,128)S(1)} %bitcast.7, f32[16,1,128]{2,1,0:T(1,128)S(1)} %all_to_all.17.sums), custom_call_target="tpu_custom_call" | custom-call | tf_op jit(solution)/shard_map/finish/pallas_call | solution.py:260
  (2 shorter events, 0.0 us)
Async XLA Ops:
  21.8 13.7 %collective-permute-start = (f32[272,128]{1,0:T(8,128)S(1)}, f32[272,128]{1,0:T(8,128)S(1)}, u32[]{:S(2)}, u32[]{:S(2)}) collective-permute-start(f32[272,128]{1,0:T(8,128)S(1)} %bitcast.8), channel_id=1, source_target_pairs={{0,256},{1,1},{2,2},{3,3},{4,4},{5,5},{6,6},{7,7},{8,8},{9,9},{10,... | collective-permute-start | bytes 417800 | tf_op jit(solution)/shard_map/ppermute | solution.py:297
  31.3 0.7 %collective-permute-start.1 = (f32[16,128]{1,0:T(8,128)S(1)}, f32[16,128]{1,0:T(8,128)S(1)}, u32[]{:S(2)}, u32[]{:S(2)}) collective-permute-start(f32[16,128]{1,0:T(8,128)S(1)} %slice.3), channel_id=1, source_target_pairs={{0,0},{1,257},{2,258},{3,259},{4,260},{5,261},{6,262},{7,263},{8,2... | collective-permute-start | bytes 24584 | tf_op jit(solution)/shard_map/ppermute | solution.py:298

commit v6 on v5

--- a/solution.py
+++ b/solution.py
@@ -72,13 +72,15 @@
         g, o = g * growth[k], growth[k] * o + offset[k]
     low = lanes((LEVELS, ROWS)) < 64
     maps = (jnp.where(low, g, pltpu.roll(o, 64, 1)), jnp.where(low, pltpu.roll(g, 64, 1), o))
-    for r in range(SLAB):
-        for a in range(4):
-            x = slab[a, pl.ds(r, LEVELS, stride=SLAB), :]
-            sent[pl.ds(SENT * 2 * r + 4 * a, 4), :] = x[:4]
-            sent[pl.ds(SENT * (2 * r + 1) + 4 * a, 4), :] = x[4:]
-        for parity in range(2):
-            sent[pl.ds(SENT * (2 * r + parity) + 16, 1), :] = maps[parity][r : r + 1]
+    for half in range(HALVES):
+        for r in range(SLAB):
+            even = SENT * (RING * half + 2 * r)
+            for a in range(4):
+                x = slab[a, pl.ds(r, LEVELS, stride=SLAB), :]
+                sent[pl.ds(even + 4 * a, 4), :] = x[:4]
+                sent[pl.ds(even + SENT + 4 * a, 4), :] = x[4:]
+            for parity in range(2):
+                sent[pl.ds(even + SENT * parity + 16, 1), :] = maps[parity][r : r + 1]
     for copy in rows:
         copy.wait()
 
@@ -88,7 +90,7 @@
     return pl.pallas_call(
         pack_kernel,
         out_shape=(
-            pltpu.VMEM((RING * SENT, 128), f32),
+            pltpu.VMEM((HALVES * RING * SENT, 128), f32),
             pltpu.VMEM((CELLS * LEVELS, ROWS), f32),
             pltpu.VMEM((CELLS * LEVELS, ROWS), f32),
             pltpu.VMEM((2 * SEGMENTS, LEVELS, ROWS), f32),
@@ -107,17 +109,16 @@
     )(tracer, courant, hops, area)
 
 
-def solve_kernel(hops, area, own, far, far_maps, back, source, courant, source_t, courant_t):
+def solve_kernel(hops, area, got, back, source, courant, source_t, courant_t):
     half = lax.axis_index("half")
     ring = lax.axis_index("ring")
     polar, start = polar_start()
     row, parity = ring // 2, ring % 2
     for d in range(HALVES * RING):
-        ref, base = (own if d < RING else far), (d % RING) * SENT
         for side in range(2):
             to = pl.ds(side * 128, 128)
-            source[pl.ds(4 * d, 4), to] = ref[pl.ds(base + 4 * side, 4), :]
-            courant[pl.ds(4 * d, 4), to] = ref[pl.ds(base + 8 + 4 * side, 4), :]
+            source[pl.ds(4 * d, 4), to] = got[pl.ds(SENT * d + 4 * side, 4), :]
+            courant[pl.ds(4 * d, 4), to] = got[pl.ds(SENT * d + 8 + 4 * side, 4), :]
     lane = lanes((1, 128))
     slab_row = lane == start + row
     hop = jnp.sum(jnp.where(slab_row, hops[...].astype(jnp.float32), 0.0), axis=1, keepdims=True).astype(jnp.int32)
@@ -164,8 +165,7 @@
             source_t[at, :] = u
             flux[k] = c * u
     source[...] = source_t[...].T
-    at = pl.ds(16, RING, stride=SENT)
-    x = jnp.concatenate([own[at, :], jnp.where(polar, far[at, :], far_maps[...])], 0)
+    x = got[pl.ds(16, HALVES * RING, stride=SENT), :]
     low = lanes(x.shape) < 64
     turned = pltpu.roll(x, 64, 1)
     rest_g = jnp.where(low, x, turned)
@@ -174,35 +174,36 @@
         rest_o = rest_g * pltpu.roll(rest_o, stride, 0) + rest_o
         rest_g = rest_g * pltpu.roll(rest_g, stride, 0)
     rest = pltpu.roll(rest_o / (1.0 - rest_g), 1, 0)
-    wrap = jnp.where(half == 0, rest[:1], rest[RING : RING + 1])
     areas = area[...]
     mine = lane // 64 == parity
     in_slab = polar & (lane >= start) & (lane < start + SLAB)
-    weighted = jnp.where(mine & ~in_slab, areas, 0.0) * wrap
+    weighted = jnp.where(mine & ~in_slab, areas, 0.0) * rest[:1]
     weighted = jnp.sum(weighted, axis=1, keepdims=True)
     slab_area = jnp.sum(jnp.where(polar & slab_row, areas, 0.0), axis=1, keepdims=True)
-    loops = pltpu.roll(inflow, (4 * parity + 128 - 64 * half) % 128, 1) * slab_area
+    loops = pltpu.roll(inflow, 4 * parity, 1) * slab_area
     sums = jnp.where(lane == row, weighted, 0.0)
     sums = sums + jnp.where((lane >= 4 * parity) & (lane < 4 * parity + 4), loops, 0.0)
     total = jnp.sum(areas, axis=1, keepdims=True)
     sums = jnp.where(lane == 8, jnp.where(ring == 0, total, 0.0), sums)
     for d in range(RING):
         for side in range(2):
-            back[pl.ds(BACK * d + 4 * side, 4), :] = source[pl.ds(4 * d, 4), pl.ds(side * 128, 128)]
-        back[pl.ds(BACK * d + 8, 1), :] = rest[d : d + 1]
+            to = pl.ds(side * 128, 128)
+            solved = [source[pl.ds(4 * (d + first), 4), to] for first in (0, RING)]
+            back[pl.ds(BACK * d + 4 * side, 4), :] = jnp.where(half == 0, *solved)
+        back[pl.ds(BACK * d + 8, 1), :] = jnp.where(half == 0, rest[d : d + 1], rest[d + RING : d + RING + 1])
         back[pl.ds(BACK * d + 9, 1), :] = sums
 
 
-def solve(hops, area, own, far, far_maps):
+def solve(hops, area, got):
     f32 = jnp.float32
     return pl.pallas_call(
         solve_kernel,
         out_shape=pltpu.VMEM((RING * BACK, 128), f32),
-        in_specs=[VMEM] * 5,
+        in_specs=[VMEM] * 3,
         out_specs=VMEM,
         scratch_shapes=[pltpu.VMEM((ROWS, CELLS), f32)] * 2 + [pltpu.VMEM((CELLS, ROWS), f32)] * 2,
         name="solve",
-    )(*in_vmem(hops, area, own, far, far_maps))
+    )(*in_vmem(hops, area, got))
 
 
 def spread_kernel(got, sums):
@@ -214,14 +215,32 @@
 def spread(got, lats):
     return pl.pallas_call(
         spread_kernel,
-        out_shape=pltpu.VMEM((lats, 1, 128), jnp.float32),
+        out_shape=jax.ShapeDtypeStruct((lats, 1, 128), jnp.float32),
         in_specs=[VMEM],
         out_specs=VMEM,
         name="spread",
     )(*in_vmem(got))
 
 
-def finish_kernel(source_t, courant_t, entries, got, sums, updated, mean, updated_t, level, sems):
+def mean_kernel(sums, mean):
+    total = sums[0]
+    for i in range(1, sums.shape[0]):
+        total = total + sums[i]
+    area = jnp.sum(jnp.where(lanes((1, 128)) == 8, total, 0.0), axis=1, keepdims=True)
+    mean[...] = (total / area)[0, :LEVELS]
+
+
+def mean(sums):
+    return pl.pallas_call(
+        mean_kernel,
+        out_shape=jax.ShapeDtypeStruct((LEVELS,), jnp.float32),
+        in_specs=[VMEM],
+        out_specs=VMEM,
+        name="mean",
+    )(*in_vmem(sums))
+
+
+def finish_kernel(source_t, courant_t, entries, got, updated, updated_t, level, sems):
     low = lanes((LEVELS, ROWS)) < 64
     even = got[pl.ds(8, LEVELS, stride=2 * BACK), :]
     odd = got[pl.ds(8 + BACK, LEVELS, stride=2 * BACK), :]
@@ -246,60 +265,38 @@
             level[l, rows, to] = jnp.where(polar, solved, level[l, rows, to])
         copies.append(pltpu.make_async_copy(level.at[l], updated.at[l], sems.at[l]))
         copies[l].start()
-    total = sums[0]
-    for i in range(1, sums.shape[0]):
-        total = total + sums[i]
-    area = jnp.sum(jnp.where(lanes((1, 128)) == 8, total, 0.0), axis=1, keepdims=True)
-    mean[...] = (total / area)[0, :LEVELS]
     for copy in copies:
         copy.wait()
 
 
-def finish(source_t, courant_t, entries, got, sums):
+def finish(source_t, courant_t, entries, got):
     f32 = jnp.float32
     return pl.pallas_call(
         finish_kernel,
-        out_shape=(
-            jax.ShapeDtypeStruct((LEVELS, ROWS, CELLS), f32),
-            jax.ShapeDtypeStruct((LEVELS,), f32),
-        ),
-        in_specs=[VMEM] * 5,
-        out_specs=(pl.BlockSpec(memory_space=pl.ANY), VMEM),
+        out_shape=jax.ShapeDtypeStruct((LEVELS, ROWS, CELLS), f32),
+        in_specs=[VMEM] * 4,
+        out_specs=pl.BlockSpec(memory_space=pl.ANY),
         scratch_shapes=[
             pltpu.VMEM((CELLS * LEVELS, ROWS), f32),
             pltpu.VMEM((LEVELS, ROWS, CELLS), f32),
             pltpu.SemaphoreType.DMA((LEVELS,)),
         ],
         name="finish",
-    )(*in_vmem(source_t, courant_t, entries, got, sums))
-
-
-def exchange(rows):
-    blocks = rows.reshape(RING, -1, 1, 128)
-    return lax.all_to_all(blocks, "ring", 0, 0, tiled=True).reshape(rows.shape)
+    )(*in_vmem(source_t, courant_t, entries, got))
+
+
+def exchange(rows, axes):
+    blocks = rows.reshape(lax.axis_size(axes), -1, 1, 128)
+    return lax.all_to_all(blocks, axes, 0, 0, tiled=True).reshape(rows.shape)
 
 
 def body(tracer, courant, hop_counts, row_area):
-    lats = lax.axis_size("lat")
-
-    def across(polar):
-        half = RING * lats
-        pairs = []
-        for i in range(HALVES * half):
-            moved = (i % lats in (0, lats - 1)) == polar
-            pairs.append((i, (i + half) % (HALVES * half) if moved else i))
-        return pairs
-
     hops, area = hop_counts.reshape(1, ROWS), row_area.reshape(1, ROWS)
     sent, source_t, courant_t, entries, hops, area = pack(tracer, courant, hops, area)
-    got = exchange(sent)
-    every = ("half", "ring", "lat")
-    far = lax.ppermute(got, every, across(True))
-    far_maps = lax.ppermute(lax.slice(got, (16, 0), (RING * SENT, 128), (SENT, 1)), every, across(False))
-    back = solve(hops, area, got, far, far_maps)
-    back = exchange(back)
-    sums = lax.all_to_all(spread(back, lats), "lat", 0, 0, tiled=True)
-    return finish(source_t, courant_t, entries, back, sums)
+    got = exchange(sent, ("half", "ring"))
+    back = exchange(solve(hops, area, got), "ring")
+    sums = lax.all_to_all(spread(back, lax.axis_size("lat")), "lat", 0, 0, tiled=True)
+    return finish(source_t, courant_t, entries, back), mean(sums)
 
 
 def solution(mesh):

time: 62.8 us -> 64.5 us (1.027)
  starting transfers between devices: 10.2 us -> 6.85 us
  blocking collectives: 42.7 us -> 45.2 us
  waiting for transfers between devices: 3.51 us -> 5.41 us
  Pallas kernels: 5.46 us -> 6.15 us
    ppermute x2 -> x0, starting transfers between devices: 10.2 us -> none  [the longest x1 9.49 us: body(): far = lax.ppermute(got, every, across(True))]
    all_to_all x0 -> x1, starting transfers between devices: none -> 6.85 us  [body(): lax.all_to_all(spread(back, lax.axis_size('lat')), 'lat', 0, 0, tiled=True)]
    all_to_all x0 -> x1, waiting for transfers between devices: none -> 5.41 us  [body(): lax.all_to_all(spread(back, lax.axis_size('lat')), 'lat', 0, 0, tiled=True)]
    ppermute x2 -> x0, waiting for transfers between devices: 3.51 us -> none  [the longest x1 3.5 us: body(): far = lax.ppermute(got, every, across(True))]
    all_to_all x3 -> x2, blocking collectives: 42.7 us -> 45.2 us  [exchange(): return lax.all_to_all(blocks, axes, 0, 0, tiled=True).reshape(rows.shape)]
    pallas_call x3 -> x4, Pallas kernels: 4.45 us -> 5.15 us  [the longest x1 2.57 us: pack(): pl.pallas_call(pack_kernel, out_shape=(pltpu.VMEM((HALVES * RING * SENT,...]
  transfers between devices with their start and end apart: 2 -> 1, of which waited for: 1 -> 1; matrix products, arithmetic and copies ran while one was open for 0% -> 0% of each run, Pallas kernels for 0% -> 2%
where the time goes in v6:
time: 64.5 us; the launch traced here: 64.2 us
  blocking collectives  45.2 us (70%)
  starting transfers between devices  6.85 us (11%)
  Pallas kernels  6.15 us (10%)
  waiting for transfers between devices  5.41 us (8%)
  between operations  0.66 us (1%)
    all_to_all x2, blocking collectives, exchange(): return lax.all_to_all(blocks, axes, 0, 0, tiled=True).reshape(rows.shape)  45.2 us
    all_to_all x1, starting transfers between devices, body(): lax.all_to_all(spread(back, lax.axis_size('lat')), 'lat', 0, 0, tiled=True)  6.85 us
    all_to_all x1, waiting for transfers between devices, body(): lax.all_to_all(spread(back, lax.axis_size('lat')), 'lat', 0, 0, tiled=True)  5.41 us
    pallas_call x1, Pallas kernels, pack(): pl.pallas_call(pack_kernel, out_shape=(pltpu.VMEM((HALVES * RING * SENT,...  2.57 us
    pallas_call x1, Pallas kernels, finish(): pl.pallas_call(finish_kernel, out_shape=jax.ShapeDtypeStruct((LEVELS, ROW...  1.37 us
  transfers between devices with their start and end apart: 1, of which 1 were waited for; matrix products, arithmetic and copies ran while one was open for 0% of the time, Pallas kernels for 2%

profile of v6, /device:TPU:1, one launch (start us, length us, event | category | flops | bytes accessed | tf_op | source)
XLA Modules:
  0.0 64.2 jit_solution(10299928697918760657)
XLA Ops:
  0.6 2.6 %pack.1 = (f32[544,128]{1,0:T(8,128)S(1)}, f32[2048,128]{1,0:T(8,128)S(1)}, f32[2048,128]{1,0:T(8,128)S(1)}, f32[16,8,128]{2,1,0:T(8,128)S(1)}, s32[1,128]{1,0:T(1,128)S(1)}, /*index=5*/f32[1,128]{1,0:T(1,128)S(1)}) custom-call(f32[8,128,256]{2,1,0:T(8,128)} %tracer.1, f32[8,128,256]{2,1,0:T(8,128)} %courant.1, s32[1,128]{1,0:T(1,128)} %bitcast.11, ...), custom_call_target="tpu_custom_call" | custom-call | tf_op jit(solution)/shard_map/pack/pallas_call | solution.py:90
  3.2 33.1 %all_to_all.15 = f32[32,17,1,128]{3,2,1,0:T(1,128)S(1)} all-to-all(f32[32,17,1,128]{3,2,1,0:T(1,128)S(1)} %bitcast.10), channel_id=1, replica_groups=mesh['half'=2,'ring'=16,'lat'=16] {'half','ring'}, dimensions={0} | all-to-all | bytes 557056 | tf_op jit(solution)/shard_map/all_to_all | solution.py:290
  36.3 1.0 %solve.1 = f32[160,128]{1,0:T(8,128)S(1)} custom-call(s32[1,128]{1,0:T(1,128)S(1)} %get-tuple-element.11.hops, f32[1,128]{1,0:T(1,128)S(1)} %get-tuple-element.12.area, f32[544,128]{1,0:T(8,128)S(1)} %bitcast.6), custom_call_target="tpu_custom_call" | custom-call | tf_op jit(solution)/shard_map/solve/pallas_call | solution.py:199
  37.3 12.1 %all_to_all.16 = f32[16,10,1,128]{3,2,1,0:T(1,128)S(1)} all-to-all(f32[16,10,1,128]{3,2,1,0:T(1,128)S(1)} %bitcast.9), channel_id=1, replica_groups=mesh['half'=2,'ring'=16,'lat'=16] {'ring'}, dimensions={0} | all-to-all | bytes 163840 | tf_op jit(solution)/shard_map/all_to_all | solution.py:290
  49.4 0.6 spread.1
  50.0 6.8 %all-to-all-start.2 = ((f32[16,1,128]{2,1,0:T(1,128)}), f32[16,1,128]{2,1,0:T(1,128)S(1)}, u32[]{:S(2)}, u32[]{:S(2)}) async-start(f32[16,1,128]{2,1,0:T(1,128)} %spread.1), calls=%async_computation.2 | async-start | bytes 16384 | tf_op jit(solution)/shard_map/all_to_all | solution.py:298
  56.9 1.4 %finish.1 = f32[8,128,256]{2,1,0:T(8,128)} custom-call(f32[2048,128]{1,0:T(8,128)S(1)} %get-tuple-element.8.source_t, f32[2048,128]{1,0:T(8,128)S(1)} %get-tuple-element.9.courant_t, f32[16,8,128]{2,1,0:T(8,128)S(1)} %get-tuple-element.10.entries, f32[160,128]{1,0:T(8,128)S(1)} %bitcast.8), custom_call_target="tpu_custom_call" | custom-call | tf_op jit(solution)/shard_map/finish/pallas_call | solution.py:274
  58.2 5.4 %all-to-all-done.2.sums = f32[16,1,128]{2,1,0:T(1,128)S(1)} async-done(((f32[16,1,128]{2,1,0:T(1,128)}), f32[16,1,128]{2,1,0:T(1,128)S(1)}, u32[]{:S(2)}, u32[]{:S(2)}) %all-to-all-start.2) | async-done | bytes 8224 | tf_op jit(solution)/shard_map/all_to_all | solution.py:298
  63.6 0.6 mean.1
Async XLA Ops:
  50.0 13.6 %all-to-all-start.2 = ((f32[16,1,128]{2,1,0:T(1,128)}), f32[16,1,128]{2,1,0:T(1,128)S(1)}, u32[]{:S(2)}, u32[]{:S(2)}) async-start(f32[16,1,128]{2,1,0:T(1,128)} %spread.1), calls=%async_computation.2 | async-start | bytes 16384 | tf_op jit(solution)/shard_map/all_to_all | solution.py:298

commit v7 on v5

--- a/solution.py
+++ b/solution.py
@@ -214,14 +214,32 @@
 def spread(got, lats):
     return pl.pallas_call(
         spread_kernel,
-        out_shape=pltpu.VMEM((lats, 1, 128), jnp.float32),
+        out_shape=jax.ShapeDtypeStruct((lats, 1, 128), jnp.float32),
         in_specs=[VMEM],
         out_specs=VMEM,
         name="spread",
     )(*in_vmem(got))
 
 
-def finish_kernel(source_t, courant_t, entries, got, sums, updated, mean, updated_t, level, sems):
+def mean_kernel(sums, mean):
+    total = sums[0]
+    for i in range(1, sums.shape[0]):
+        total = total + sums[i]
+    area = jnp.sum(jnp.where(lanes((1, 128)) == 8, total, 0.0), axis=1, keepdims=True)
+    mean[...] = (total / area)[0, :LEVELS]
+
+
+def mean(sums):
+    return pl.pallas_call(
+        mean_kernel,
+        out_shape=jax.ShapeDtypeStruct((LEVELS,), jnp.float32),
+        in_specs=[VMEM],
+        out_specs=VMEM,
+        name="mean",
+    )(*in_vmem(sums))
+
+
+def finish_kernel(source_t, courant_t, entries, got, updated, updated_t, level, sems):
     low = lanes((LEVELS, ROWS)) < 64
     even = got[pl.ds(8, LEVELS, stride=2 * BACK), :]
     odd = got[pl.ds(8 + BACK, LEVELS, stride=2 * BACK), :]
@@ -246,32 +264,24 @@
             level[l, rows, to] = jnp.where(polar, solved, level[l, rows, to])
         copies.append(pltpu.make_async_copy(level.at[l], updated.at[l], sems.at[l]))
         copies[l].start()
-    total = sums[0]
-    for i in range(1, sums.shape[0]):
-        total = total + sums[i]
-    area = jnp.sum(jnp.where(lanes((1, 128)) == 8, total, 0.0), axis=1, keepdims=True)
-    mean[...] = (total / area)[0, :LEVELS]
     for copy in copies:
         copy.wait()
 
 
-def finish(source_t, courant_t, entries, got, sums):
+def finish(source_t, courant_t, entries, got):
     f32 = jnp.float32
     return pl.pallas_call(
         finish_kernel,
-        out_shape=(
-            jax.ShapeDtypeStruct((LEVELS, ROWS, CELLS), f32),
-            jax.ShapeDtypeStruct((LEVELS,), f32),
-        ),
-        in_specs=[VMEM] * 5,
-        out_specs=(pl.BlockSpec(memory_space=pl.ANY), VMEM),
+        out_shape=jax.ShapeDtypeStruct((LEVELS, ROWS, CELLS), f32),
+        in_specs=[VMEM] * 4,
+        out_specs=pl.BlockSpec(memory_space=pl.ANY),
         scratch_shapes=[
             pltpu.VMEM((CELLS * LEVELS, ROWS), f32),
             pltpu.VMEM((LEVELS, ROWS, CELLS), f32),
             pltpu.SemaphoreType.DMA((LEVELS,)),
         ],
         name="finish",
-    )(*in_vmem(source_t, courant_t, entries, got, sums))
+    )(*in_vmem(source_t, courant_t, entries, got))
 
 
 def exchange(rows):
@@ -299,7 +309,7 @@
     back = solve(hops, area, got, far, far_maps)
     back = exchange(back)
     sums = lax.all_to_all(spread(back, lats), "lat", 0, 0, tiled=True)
-    return finish(source_t, courant_t, entries, back, sums)
+    return finish(source_t, courant_t, entries, back), mean(sums)
 
 
 def solution(mesh):

time: 62.8 us -> 62.3 us (level)
  blocking collectives: 42.7 us -> 29.7 us
  starting transfers between devices: 10.2 us -> 16.6 us
  waiting for transfers between devices: 3.51 us -> 8.92 us
  Pallas kernels: 5.46 us -> 6.15 us
    all_to_all x1 -> x0, blocking collectives: 13.1 us -> none  [body(): sums = lax.all_to_all(spread(back, lats), 'lat', 0, 0, tiled=True)]
    all_to_all x0 -> x1, starting transfers between devices: none -> 6.49 us  [body(): sums = lax.all_to_all(spread(back, lats), 'lat', 0, 0, tiled=True)]
    all_to_all x0 -> x1, waiting for transfers between devices: none -> 5.41 us  [body(): sums = lax.all_to_all(spread(back, lats), 'lat', 0, 0, tiled=True)]
    pallas_call x2 -> x3, Pallas kernels: 1.89 us -> 2.59 us  [the longest x1 1.37 us: finish(): pl.pallas_call(finish_kernel, out_shape=jax.ShapeDtypeStruct((LEVELS, ROW...]
  transfers between devices with their start and end apart: 2 -> 3, of which waited for: 1 -> 2; matrix products, arithmetic and copies ran while one was open for 0% -> 0% of each run, Pallas kernels for 0% -> 2%
where the time goes in v7:
time: 62.3 us; the launch traced here: 62.1 us
  blocking collectives  29.7 us (48%)
  starting transfers between devices  16.6 us (27%)
  waiting for transfers between devices  8.92 us (14%)
  Pallas kernels  6.15 us (10%)
  between operations  0.69 us (1%)
    all_to_all x2, blocking collectives, exchange(): return lax.all_to_all(blocks, 'ring', 0, 0, tiled=True).reshape(rows.shape)  29.7 us
    ppermute x1, starting transfers between devices, body(): far = lax.ppermute(got, every, across(True))  9.49 us
    all_to_all x1, starting transfers between devices, body(): sums = lax.all_to_all(spread(back, lats), 'lat', 0, 0, tiled=True)  6.49 us
    all_to_all x1, waiting for transfers between devices, body(): sums = lax.all_to_all(spread(back, lats), 'lat', 0, 0, tiled=True)  5.41 us
    ppermute x1, waiting for transfers between devices, body(): far = lax.ppermute(got, every, across(True))  3.5 us
    pallas_call x1, Pallas kernels, pack(): pl.pallas_call(pack_kernel, out_shape=(pltpu.VMEM((RING * SENT, 128), f32...  2.56 us
    pallas_call x1, Pallas kernels, finish(): pl.pallas_call(finish_kernel, out_shape=jax.ShapeDtypeStruct((LEVELS, ROW...  1.37 us
  transfers between devices with their start and end apart: 3, of which 2 were waited for; matrix products, arithmetic and copies ran while one was open for 0% of the time, Pallas kernels for 2%

profile of v7, /device:TPU:1, one launch (start us, length us, event | category | flops | bytes accessed | tf_op | source)
XLA Modules:
  0.0 62.1 jit_solution(9168412018368334806)
XLA Ops:
  0.6 2.6 %pack.1 = (f32[272,128]{1,0:T(8,128)S(1)}, f32[2048,128]{1,0:T(8,128)S(1)}, f32[2048,128]{1,0:T(8,128)S(1)}, f32[16,8,128]{2,1,0:T(8,128)S(1)}, s32[1,128]{1,0:T(1,128)S(1)}, /*index=5*/f32[1,128]{1,0:T(1,128)S(1)}) custom-call(f32[8,128,256]{2,1,0:T(8,128)} %tracer.1, f32[8,128,256]{2,1,0:T(8,128)} %courant.1, s32[1,128]{1,0:T(1,128)} %bitcast.13, ...), custom_call_target="tpu_custom_call" | custom-call | tf_op jit(solution)/shard_map/pack/pallas_call | solution.py:88
  3.2 18.6 %all_to_all.15 = f32[16,17,1,128]{3,2,1,0:T(1,128)S(1)} all-to-all(f32[16,17,1,128]{3,2,1,0:T(1,128)S(1)} %bitcast.12), channel_id=1, replica_groups=mesh['half'=2,'ring'=16,'lat'=16] {'ring'}, dimensions={0} | all-to-all | bytes 278528 | tf_op jit(solution)/shard_map/all_to_all | solution.py:289
  21.8 9.5 %collective-permute-start = (f32[272,128]{1,0:T(8,128)S(1)}, f32[272,128]{1,0:T(8,128)S(1)}, u32[]{:S(2)}, u32[]{:S(2)}) collective-permute-start(f32[272,128]{1,0:T(8,128)S(1)} %bitcast.8), channel_id=1, source_target_pairs={{0,256},{1,1},{2,2},{3,3},{4,4},{5,5},{6,6},{7,7},{8,8},{9,9},{10,... | collective-permute-start | bytes 417800 | tf_op jit(solution)/shard_map/ppermute | solution.py:307
  31.3 0.7 %collective-permute-start.1 = (f32[16,128]{1,0:T(8,128)S(1)}, f32[16,128]{1,0:T(8,128)S(1)}, u32[]{:S(2)}, u32[]{:S(2)}) collective-permute-start(f32[16,128]{1,0:T(8,128)S(1)} %slice.3), channel_id=1, source_target_pairs={{0,0},{1,257},{2,258},{3,259},{4,260},{5,261},{6,262},{7,263},{8,2... | collective-permute-start | bytes 24584 | tf_op jit(solution)/shard_map/ppermute | solution.py:308
  32.0 0.0 collective-permute-done.1.far_maps
  32.0 3.5 %collective-permute-done.far = f32[272,128]{1,0:T(8,128)S(1)} collective-permute-done((f32[272,128]{1,0:T(8,128)S(1)}, f32[272,128]{1,0:T(8,128)S(1)}, u32[]{:S(2)}, u32[]{:S(2)}) %collective-permute-start) | collective-permute-done | bytes 139296 | tf_op jit(solution)/shard_map/ppermute | solution.py:307
  35.5 1.0 %solve.1 = f32[160,128]{1,0:T(8,128)S(1)} custom-call(s32[1,128]{1,0:T(1,128)S(1)} %get-tuple-element.11.hops, f32[1,128]{1,0:T(1,128)S(1)} %get-tuple-element.12.area, f32[272,128]{1,0:T(8,128)S(1)} %bitcast.10, f32[272,128]{1,0:T(8,128)S(1)} %collective-permute-done.far, f32[16,128]{1,0:T(8,128)S(1)} %collective-permute-done.1.far_maps), custom_call_target="tpu_custom_call" | custom-call | tf_op jit(solution)/shard_map/solve/pallas_call | solution.py:198
  36.5 11.1 %all_to_all.16 = f32[16,10,1,128]{3,2,1,0:T(1,128)S(1)} all-to-all(f32[16,10,1,128]{3,2,1,0:T(1,128)S(1)} %bitcast.11), channel_id=1, replica_groups=mesh['half'=2,'ring'=16,'lat'=16] {'ring'}, dimensions={0} | all-to-all | bytes 163840 | tf_op jit(solution)/shard_map/all_to_all | solution.py:289
  47.6 0.6 spread.1
  48.2 6.5 %all-to-all-start.2 = ((f32[16,1,128]{2,1,0:T(1,128)}), f32[16,1,128]{2,1,0:T(1,128)S(1)}, u32[]{:S(2)}, u32[]{:S(2)}) async-start(f32[16,1,128]{2,1,0:T(1,128)} %spread.1), calls=%async_computation.2 | async-start | bytes 16384 | tf_op jit(solution)/shard_map/all_to_all | solution.py:311
  54.7 1.4 %finish.1 = f32[8,128,256]{2,1,0:T(8,128)} custom-call(f32[2048,128]{1,0:T(8,128)S(1)} %get-tuple-element.8.source_t, f32[2048,128]{1,0:T(8,128)S(1)} %get-tuple-element.9.courant_t, f32[16,8,128]{2,1,0:T(8,128)S(1)} %get-tuple-element.10.entries, f32[160,128]{1,0:T(8,128)S(1)} %bitcast.7), custom_call_target="tpu_custom_call" | custom-call | tf_op jit(solution)/shard_map/finish/pallas_call | solution.py:273
  56.0 5.4 %all-to-all-done.2.sums = f32[16,1,128]{2,1,0:T(1,128)S(1)} async-done(((f32[16,1,128]{2,1,0:T(1,128)}), f32[16,1,128]{2,1,0:T(1,128)S(1)}, u32[]{:S(2)}, u32[]{:S(2)}) %all-to-all-start.2) | async-done | bytes 8224 | tf_op jit(solution)/shard_map/all_to_all | solution.py:311
  61.5 0.6 mean.1
  (1 shorter events, 0.0 us)
Async XLA Ops:
  21.8 13.7 %collective-permute-start = (f32[272,128]{1,0:T(8,128)S(1)}, f32[272,128]{1,0:T(8,128)S(1)}, u32[]{:S(2)}, u32[]{:S(2)}) collective-permute-start(f32[272,128]{1,0:T(8,128)S(1)} %bitcast.8), channel_id=1, source_target_pairs={{0,256},{1,1},{2,2},{3,3},{4,4},{5,5},{6,6},{7,7},{8,8},{9,9},{10,... | collective-permute-start | bytes 417800 | tf_op jit(solution)/shard_map/ppermute | solution.py:307
  31.3 0.7 %collective-permute-start.1 = (f32[16,128]{1,0:T(8,128)S(1)}, f32[16,128]{1,0:T(8,128)S(1)}, u32[]{:S(2)}, u32[]{:S(2)}) collective-permute-start(f32[16,128]{1,0:T(8,128)S(1)} %slice.3), channel_id=1, source_target_pairs={{0,0},{1,257},{2,258},{3,259},{4,260},{5,261},{6,262},{7,263},{8,2... | collective-permute-start | bytes 24584 | tf_op jit(solution)/shard_map/ppermute | solution.py:308
  48.2 13.3 %all-to-all-start.2 = ((f32[16,1,128]{2,1,0:T(1,128)}), f32[16,1,128]{2,1,0:T(1,128)S(1)}, u32[]{:S(2)}, u32[]{:S(2)}) async-start(f32[16,1,128]{2,1,0:T(1,128)} %spread.1), calls=%async_computation.2 | async-start | bytes 16384 | tf_op jit(solution)/shard_map/all_to_all | solution.py:311

commit v8 on v7

--- a/solution.py
+++ b/solution.py
@@ -62,7 +62,7 @@
         for k in range(SEGMENTS):
             at = pl.ds(LEVELS * (STEPS * k + step), LEVELS)
             c = courant_t[at, :]
-            f = c * (1.0 / (1.0 + c))
+            f = 1.0 - 1.0 / (1.0 + c)
             offset[k] = f * (source_t[at, :] + offset[k])
             growth[k] = growth[k] * f
     g, o = growth[0], offset[0]
@@ -133,7 +133,7 @@
         for k in parts:
             at = pl.ds(64 * k + step, 8, stride=8)
             c = courant_t[at, :]
-            f = c * (1.0 / (1.0 + c))
+            f = 1.0 - 1.0 / (1.0 + c)
             offset[k] = f * (source_t[at, :] + offset[k])
             growth[k] = growth[k] * f
     place = lax.broadcasted_iota(jnp.int32, (8, ROWS), 0)

time: 62.3 us -> 62.4 us (level)
  no operation moved by 1% of the time
where the time goes in v8:
time: 62.4 us; the launch traced here: 62.1 us
  blocking collectives  29.7 us (48%)
  starting transfers between devices  16.6 us (27%)
  waiting for transfers between devices  8.92 us (14%)
  Pallas kernels  6.17 us (10%)
  between operations  0.69 us (1%)
    all_to_all x2, blocking collectives, exchange(): return lax.all_to_all(blocks, 'ring', 0, 0, tiled=True).reshape(rows.shape)  29.7 us
    ppermute x1, starting transfers between devices, body(): far = lax.ppermute(got, every, across(True))  9.49 us
    all_to_all x1, starting transfers between devices, body(): sums = lax.all_to_all(spread(back, lats), 'lat', 0, 0, tiled=True)  6.49 us
    all_to_all x1, waiting for transfers between devices, body(): sums = lax.all_to_all(spread(back, lats), 'lat', 0, 0, tiled=True)  5.41 us
    ppermute x1, waiting for transfers between devices, body(): far = lax.ppermute(got, every, across(True))  3.5 us
    pallas_call x1, Pallas kernels, pack(): pl.pallas_call(pack_kernel, out_shape=(pltpu.VMEM((RING * SENT, 128), f32...  2.59 us
    pallas_call x1, Pallas kernels, finish(): pl.pallas_call(finish_kernel, out_shape=jax.ShapeDtypeStruct((LEVELS, ROW...  1.37 us
  transfers between devices with their start and end apart: 3, of which 2 were waited for; matrix products, arithmetic and copies ran while one was open for 0% of the time, Pallas kernels for 2%

profile of v8, /device:TPU:1, one launch (start us, length us, event | category | flops | bytes accessed | tf_op | source)
XLA Modules:
  0.0 62.1 jit_solution(17481356899073613992)
XLA Ops:
  0.6 2.6 %pack.1 = (f32[272,128]{1,0:T(8,128)S(1)}, f32[2048,128]{1,0:T(8,128)S(1)}, f32[2048,128]{1,0:T(8,128)S(1)}, f32[16,8,128]{2,1,0:T(8,128)S(1)}, s32[1,128]{1,0:T(1,128)S(1)}, /*index=5*/f32[1,128]{1,0:T(1,128)S(1)}) custom-call(f32[8,128,256]{2,1,0:T(8,128)} %tracer.1, f32[8,128,256]{2,1,0:T(8,128)} %courant.1, s32[1,128]{1,0:T(1,128)} %bitcast.13, ...), custom_call_target="tpu_custom_call" | custom-call | tf_op jit(solution)/shard_map/pack/pallas_call | solution.py:88
  3.2 18.6 %all_to_all.15 = f32[16,17,1,128]{3,2,1,0:T(1,128)S(1)} all-to-all(f32[16,17,1,128]{3,2,1,0:T(1,128)S(1)} %bitcast.12), channel_id=1, replica_groups=mesh['half'=2,'ring'=16,'lat'=16] {'ring'}, dimensions={0} | all-to-all | bytes 278528 | tf_op jit(solution)/shard_map/all_to_all | solution.py:289
  21.8 9.5 %collective-permute-start = (f32[272,128]{1,0:T(8,128)S(1)}, f32[272,128]{1,0:T(8,128)S(1)}, u32[]{:S(2)}, u32[]{:S(2)}) collective-permute-start(f32[272,128]{1,0:T(8,128)S(1)} %bitcast.8), channel_id=1, source_target_pairs={{0,256},{1,1},{2,2},{3,3},{4,4},{5,5},{6,6},{7,7},{8,8},{9,9},{10,... | collective-permute-start | bytes 417800 | tf_op jit(solution)/shard_map/ppermute | solution.py:307
  31.3 0.7 %collective-permute-start.1 = (f32[16,128]{1,0:T(8,128)S(1)}, f32[16,128]{1,0:T(8,128)S(1)}, u32[]{:S(2)}, u32[]{:S(2)}) collective-permute-start(f32[16,128]{1,0:T(8,128)S(1)} %slice.3), channel_id=1, source_target_pairs={{0,0},{1,257},{2,258},{3,259},{4,260},{5,261},{6,262},{7,263},{8,2... | collective-permute-start | bytes 24584 | tf_op jit(solution)/shard_map/ppermute | solution.py:308
  32.0 0.0 collective-permute-done.1.far_maps
  32.0 3.5 %collective-permute-done.far = f32[272,128]{1,0:T(8,128)S(1)} collective-permute-done((f32[272,128]{1,0:T(8,128)S(1)}, f32[272,128]{1,0:T(8,128)S(1)}, u32[]{:S(2)}, u32[]{:S(2)}) %collective-permute-start) | collective-permute-done | bytes 139296 | tf_op jit(solution)/shard_map/ppermute | solution.py:307
  35.5 1.0 %solve.1 = f32[160,128]{1,0:T(8,128)S(1)} custom-call(s32[1,128]{1,0:T(1,128)S(1)} %get-tuple-element.11.hops, f32[1,128]{1,0:T(1,128)S(1)} %get-tuple-element.12.area, f32[272,128]{1,0:T(8,128)S(1)} %bitcast.10, f32[272,128]{1,0:T(8,128)S(1)} %collective-permute-done.far, f32[16,128]{1,0:T(8,128)S(1)} %collective-permute-done.1.far_maps), custom_call_target="tpu_custom_call" | custom-call | tf_op jit(solution)/shard_map/solve/pallas_call | solution.py:198
  36.5 11.1 %all_to_all.16 = f32[16,10,1,128]{3,2,1,0:T(1,128)S(1)} all-to-all(f32[16,10,1,128]{3,2,1,0:T(1,128)S(1)} %bitcast.11), channel_id=1, replica_groups=mesh['half'=2,'ring'=16,'lat'=16] {'ring'}, dimensions={0} | all-to-all | bytes 163840 | tf_op jit(solution)/shard_map/all_to_all | solution.py:289
  47.6 0.6 spread.1
  48.2 6.5 %all-to-all-start.2 = ((f32[16,1,128]{2,1,0:T(1,128)}), f32[16,1,128]{2,1,0:T(1,128)S(1)}, u32[]{:S(2)}, u32[]{:S(2)}) async-start(f32[16,1,128]{2,1,0:T(1,128)} %spread.1), calls=%async_computation.2 | async-start | bytes 16384 | tf_op jit(solution)/shard_map/all_to_all | solution.py:311
  54.7 1.4 %finish.1 = f32[8,128,256]{2,1,0:T(8,128)} custom-call(f32[2048,128]{1,0:T(8,128)S(1)} %get-tuple-element.8.source_t, f32[2048,128]{1,0:T(8,128)S(1)} %get-tuple-element.9.courant_t, f32[16,8,128]{2,1,0:T(8,128)S(1)} %get-tuple-element.10.entries, f32[160,128]{1,0:T(8,128)S(1)} %bitcast.7), custom_call_target="tpu_custom_call" | custom-call | tf_op jit(solution)/shard_map/finish/pallas_call | solution.py:273
  56.1 5.4 %all-to-all-done.2.sums = f32[16,1,128]{2,1,0:T(1,128)S(1)} async-done(((f32[16,1,128]{2,1,0:T(1,128)}), f32[16,1,128]{2,1,0:T(1,128)S(1)}, u32[]{:S(2)}, u32[]{:S(2)}) %all-to-all-start.2) | async-done | bytes 8224 | tf_op jit(solution)/shard_map/all_to_all | solution.py:311
  61.5 0.6 mean.1
  (1 shorter events, 0.0 us)
Async XLA Ops:
  21.8 13.7 %collective-permute-start = (f32[272,128]{1,0:T(8,128)S(1)}, f32[272,128]{1,0:T(8,128)S(1)}, u32[]{:S(2)}, u32[]{:S(2)}) collective-permute-start(f32[272,128]{1,0:T(8,128)S(1)} %bitcast.8), channel_id=1, source_target_pairs={{0,256},{1,1},{2,2},{3,3},{4,4},{5,5},{6,6},{7,7},{8,8},{9,9},{10,... | collective-permute-start | bytes 417800 | tf_op jit(solution)/shard_map/ppermute | solution.py:307
  31.3 0.7 %collective-permute-start.1 = (f32[16,128]{1,0:T(8,128)S(1)}, f32[16,128]{1,0:T(8,128)S(1)}, u32[]{:S(2)}, u32[]{:S(2)}) collective-permute-start(f32[16,128]{1,0:T(8,128)S(1)} %slice.3), channel_id=1, source_target_pairs={{0,0},{1,257},{2,258},{3,259},{4,260},{5,261},{6,262},{7,263},{8,2... | collective-permute-start | bytes 24584 | tf_op jit(solution)/shard_map/ppermute | solution.py:308
  48.2 13.3 %all-to-all-start.2 = ((f32[16,1,128]{2,1,0:T(1,128)}), f32[16,1,128]{2,1,0:T(1,128)S(1)}, u32[]{:S(2)}, u32[]{:S(2)}) async-start(f32[16,1,128]{2,1,0:T(1,128)} %spread.1), calls=%async_computation.2 | async-start | bytes 16384 | tf_op jit(solution)/shard_map/all_to_all | solution.py:311

commit v9 on v8

--- a/solution.py
+++ b/solution.py
@@ -10,7 +10,7 @@
 SEGMENTS = 8
 STEPS = CELLS // SEGMENTS
 SENT = 17
-BACK = 10
+BACK = 9
 
 VMEM = pl.BlockSpec(memory_space=pltpu.VMEM)
 
@@ -30,7 +30,7 @@
 
 
 def pack_kernel(
-    tracer, courant, hops, area, sent, source_t, courant_t, entries, hops_out, area_out, source, factor, slab, sems
+    tracer, courant, hops, area, sent, source_t, courant_t, entries, hops_out, area_out, source, factor, sems
 ):
     rows = (
         pltpu.make_async_copy(hops, hops_out, sems.at[2, 0]),
@@ -54,8 +54,9 @@
         courant_t[pl.ds(l, CELLS, stride=LEVELS), :] = factor[l].T
         for side in range(2):
             across = pl.ds(128 * side, 128)
-            slab[side, pl.ds(SLAB * l, SLAB), :] = source[l, pl.ds(start, SLAB), across]
-            slab[2 + side, pl.ds(SLAB * l, SLAB), :] = factor[l, pl.ds(start, SLAB), across]
+            for a, field in enumerate((source, factor)):
+                to = pl.ds(SENT * (l // 4) + 8 * a + 4 * side + l % 4, SLAB, stride=2 * SENT)
+                sent[to, :] = field[l, pl.ds(start, SLAB), across]
     growth = [jnp.ones((LEVELS, ROWS), jnp.float32)] * SEGMENTS
     offset = [jnp.zeros((LEVELS, ROWS), jnp.float32)] * SEGMENTS
     for step in range(STEPS):
@@ -72,13 +73,9 @@
         g, o = g * growth[k], growth[k] * o + offset[k]
     low = lanes((LEVELS, ROWS)) < 64
     maps = (jnp.where(low, g, pltpu.roll(o, 64, 1)), jnp.where(low, pltpu.roll(g, 64, 1), o))
-    for r in range(SLAB):
-        for a in range(4):
-            x = slab[a, pl.ds(r, LEVELS, stride=SLAB), :]
-            sent[pl.ds(SENT * 2 * r + 4 * a, 4), :] = x[:4]
-            sent[pl.ds(SENT * (2 * r + 1) + 4 * a, 4), :] = x[4:]
+    for l in range(LEVELS):
         for parity in range(2):
-            sent[pl.ds(SENT * (2 * r + parity) + 16, 1), :] = maps[parity][r : r + 1]
+            sent[pl.ds(SENT * (2 * l + parity) + 16, 1), :] = maps[parity][l : l + 1]
     for copy in rows:
         copy.wait()
 
@@ -100,7 +97,6 @@
         scratch_shapes=[
             pltpu.VMEM((LEVELS, ROWS, CELLS), f32),
             pltpu.VMEM((LEVELS, ROWS, CELLS), f32),
-            pltpu.VMEM((4, LEVELS * SLAB, 128), f32),
             pltpu.SemaphoreType.DMA((3, LEVELS)),
         ],
         name="pack",
@@ -186,11 +182,11 @@
     sums = sums + jnp.where((lane >= 4 * parity) & (lane < 4 * parity + 4), loops, 0.0)
     total = jnp.sum(areas, axis=1, keepdims=True)
     sums = jnp.where(lane == 8, jnp.where(ring == 0, total, 0.0), sums)
+    sums = pltpu.roll(sums, 64, 1)
     for d in range(RING):
         for side in range(2):
             back[pl.ds(BACK * d + 4 * side, 4), :] = source[pl.ds(4 * d, 4), pl.ds(side * 128, 128)]
-        back[pl.ds(BACK * d + 8, 1), :] = rest[d : d + 1]
-        back[pl.ds(BACK * d + 9, 1), :] = sums
+        back[pl.ds(BACK * d + 8, 1), :] = jnp.where(lane < 64, rest[d : d + 1], sums)
 
 
 def solve(hops, area, own, far, far_maps):
@@ -206,7 +202,7 @@
 
 
 def spread_kernel(got, sums):
-    total = jnp.sum(got[pl.ds(9, RING, stride=BACK), :], axis=0, keepdims=True)
+    total = pltpu.roll(jnp.sum(got[pl.ds(8, RING, stride=BACK), :], axis=0, keepdims=True), 64, 1)
     for i in range(sums.shape[0]):
         sums[i] = total
 
@@ -243,7 +239,7 @@
     low = lanes((LEVELS, ROWS)) < 64
     even = got[pl.ds(8, LEVELS, stride=2 * BACK), :]
     odd = got[pl.ds(8 + BACK, LEVELS, stride=2 * BACK), :]
-    inflow = jnp.where(low, even, odd)
+    inflow = jnp.where(low, even, pltpu.roll(odd, 64, 1))
     flux = [inflow] + [entries[2 * k] * inflow + entries[2 * k + 1] for k in range(1, SEGMENTS)]
     for step in range(STEPS):
         for k in range(SEGMENTS):

time: 62.4 us -> 62.2 us (level)
  no operation moved by 1% of the time
where the time goes in v9:
time: 62.2 us; the launch traced here: 62 us
  blocking collectives  29.5 us (47%)
  starting transfers between devices  16.6 us (27%)
  waiting for transfers between devices  8.8 us (14%)
  Pallas kernels  6.33 us (10%)
  between operations  0.69 us (1%)
    all_to_all x2, blocking collectives, exchange(): return lax.all_to_all(blocks, 'ring', 0, 0, tiled=True).reshape(rows.shape)  29.5 us
    ppermute x1, starting transfers between devices, body(): far = lax.ppermute(got, every, across(True))  9.49 us
    all_to_all x1, starting transfers between devices, body(): sums = lax.all_to_all(spread(back, lats), 'lat', 0, 0, tiled=True)  6.49 us
    all_to_all x1, waiting for transfers between devices, body(): sums = lax.all_to_all(spread(back, lats), 'lat', 0, 0, tiled=True)  5.29 us
    ppermute x1, waiting for transfers between devices, body(): far = lax.ppermute(got, every, across(True))  3.5 us
    pallas_call x1, Pallas kernels, pack(): pl.pallas_call(pack_kernel, out_shape=(pltpu.VMEM((RING * SENT, 128), f32...  2.56 us
    pallas_call x1, Pallas kernels, finish(): pl.pallas_call(finish_kernel, out_shape=jax.ShapeDtypeStruct((LEVELS, ROW...  1.49 us
  transfers between devices with their start and end apart: 3, of which 2 were waited for; matrix products, arithmetic and copies ran while one was open for 0% of the time, Pallas kernels for 2%

profile of v9, /device:TPU:1, one launch (start us, length us, event | category | flops | bytes accessed | tf_op | source)
XLA Modules:
  0.0 62.0 jit_solution(219319270482342522)
XLA Ops:
  0.6 2.6 %pack.1 = (f32[272,128]{1,0:T(8,128)S(1)}, f32[2048,128]{1,0:T(8,128)S(1)}, f32[2048,128]{1,0:T(8,128)S(1)}, f32[16,8,128]{2,1,0:T(8,128)S(1)}, s32[1,128]{1,0:T(1,128)S(1)}, /*index=5*/f32[1,128]{1,0:T(1,128)S(1)}) custom-call(f32[8,128,256]{2,1,0:T(8,128)} %tracer.1, f32[8,128,256]{2,1,0:T(8,128)} %courant.1, s32[1,128]{1,0:T(1,128)} %bitcast.13, ...), custom_call_target="tpu_custom_call" | custom-call | tf_op jit(solution)/shard_map/pack/pallas_call | solution.py:85
  3.2 18.6 %all_to_all.15 = f32[16,17,1,128]{3,2,1,0:T(1,128)S(1)} all-to-all(f32[16,17,1,128]{3,2,1,0:T(1,128)S(1)} %bitcast.12), channel_id=1, replica_groups=mesh['half'=2,'ring'=16,'lat'=16] {'ring'}, dimensions={0} | all-to-all | bytes 278528 | tf_op jit(solution)/shard_map/all_to_all | solution.py:285
  21.8 9.5 %collective-permute-start = (f32[272,128]{1,0:T(8,128)S(1)}, f32[272,128]{1,0:T(8,128)S(1)}, u32[]{:S(2)}, u32[]{:S(2)}) collective-permute-start(f32[272,128]{1,0:T(8,128)S(1)} %bitcast.8), channel_id=1, source_target_pairs={{0,256},{1,1},{2,2},{3,3},{4,4},{5,5},{6,6},{7,7},{8,8},{9,9},{10,... | collective-permute-start | bytes 417800 | tf_op jit(solution)/shard_map/ppermute | solution.py:303
  31.3 0.7 %collective-permute-start.1 = (f32[16,128]{1,0:T(8,128)S(1)}, f32[16,128]{1,0:T(8,128)S(1)}, u32[]{:S(2)}, u32[]{:S(2)}) collective-permute-start(f32[16,128]{1,0:T(8,128)S(1)} %slice.3), channel_id=1, source_target_pairs={{0,0},{1,257},{2,258},{3,259},{4,260},{5,261},{6,262},{7,263},{8,2... | collective-permute-start | bytes 24584 | tf_op jit(solution)/shard_map/ppermute | solution.py:304
  32.0 0.0 collective-permute-done.1.far_maps
  32.0 3.5 %collective-permute-done.far = f32[272,128]{1,0:T(8,128)S(1)} collective-permute-done((f32[272,128]{1,0:T(8,128)S(1)}, f32[272,128]{1,0:T(8,128)S(1)}, u32[]{:S(2)}, u32[]{:S(2)}) %collective-permute-start) | collective-permute-done | bytes 139296 | tf_op jit(solution)/shard_map/ppermute | solution.py:303
  35.5 1.0 %solve.1 = f32[144,128]{1,0:T(8,128)S(1)} custom-call(s32[1,128]{1,0:T(1,128)S(1)} %get-tuple-element.11.hops, f32[1,128]{1,0:T(1,128)S(1)} %get-tuple-element.12.area, f32[272,128]{1,0:T(8,128)S(1)} %bitcast.10, f32[272,128]{1,0:T(8,128)S(1)} %collective-permute-done.far, f32[16,128]{1,0:T(8,128)S(1)} %collective-permute-done.1.far_maps), custom_call_target="tpu_custom_call" | custom-call | tf_op jit(solution)/shard_map/solve/pallas_call | solution.py:194
  36.5 10.9 %all_to_all.16 = f32[16,9,1,128]{3,2,1,0:T(1,128)S(1)} all-to-all(f32[16,9,1,128]{3,2,1,0:T(1,128)S(1)} %bitcast.11), channel_id=1, replica_groups=mesh['half'=2,'ring'=16,'lat'=16] {'ring'}, dimensions={0} | all-to-all | bytes 147456 | tf_op jit(solution)/shard_map/all_to_all | solution.py:285
  47.4 0.7 %spread.1 = f32[16,1,128]{2,1,0:T(1,128)} custom-call(f32[144,128]{1,0:T(8,128)S(1)} %bitcast.6), custom_call_target="tpu_custom_call" | custom-call | tf_op jit(solution)/shard_map/spread/pallas_call | solution.py:211
  48.1 6.5 %all-to-all-start.2 = ((f32[16,1,128]{2,1,0:T(1,128)}), f32[16,1,128]{2,1,0:T(1,128)S(1)}, u32[]{:S(2)}, u32[]{:S(2)}) async-start(f32[16,1,128]{2,1,0:T(1,128)} %spread.1), calls=%async_computation.2 | async-start | bytes 16384 | tf_op jit(solution)/shard_map/all_to_all | solution.py:307
  54.6 1.5 %finish.1 = f32[8,128,256]{2,1,0:T(8,128)} custom-call(f32[2048,128]{1,0:T(8,128)S(1)} %get-tuple-element.8.source_t, f32[2048,128]{1,0:T(8,128)S(1)} %get-tuple-element.9.courant_t, f32[16,8,128]{2,1,0:T(8,128)S(1)} %get-tuple-element.10.entries, f32[144,128]{1,0:T(8,128)S(1)} %bitcast.7), custom_call_target="tpu_custom_call" | custom-call | tf_op jit(solution)/shard_map/finish/pallas_call | solution.py:269
  56.1 5.3 %all-to-all-done.2.sums = f32[16,1,128]{2,1,0:T(1,128)S(1)} async-done(((f32[16,1,128]{2,1,0:T(1,128)}), f32[16,1,128]{2,1,0:T(1,128)S(1)}, u32[]{:S(2)}, u32[]{:S(2)}) %all-to-all-start.2) | async-done | bytes 8224 | tf_op jit(solution)/shard_map/all_to_all | solution.py:307
  61.3 0.6 mean.1
  (1 shorter events, 0.0 us)
Async XLA Ops:
  21.8 13.7 %collective-permute-start = (f32[272,128]{1,0:T(8,128)S(1)}, f32[272,128]{1,0:T(8,128)S(1)}, u32[]{:S(2)}, u32[]{:S(2)}) collective-permute-start(f32[272,128]{1,0:T(8,128)S(1)} %bitcast.8), channel_id=1, source_target_pairs={{0,256},{1,1},{2,2},{3,3},{4,4},{5,5},{6,6},{7,7},{8,8},{9,9},{10,... | collective-permute-start | bytes 417800 | tf_op jit(solution)/shard_map/ppermute | solution.py:303
  31.3 0.7 %collective-permute-start.1 = (f32[16,128]{1,0:T(8,128)S(1)}, f32[16,128]{1,0:T(8,128)S(1)}, u32[]{:S(2)}, u32[]{:S(2)}) collective-permute-start(f32[16,128]{1,0:T(8,128)S(1)} %slice.3), channel_id=1, source_target_pairs={{0,0},{1,257},{2,258},{3,259},{4,260},{5,261},{6,262},{7,263},{8,2... | collective-permute-start | bytes 24584 | tf_op jit(solution)/shard_map/ppermute | solution.py:304
  48.1 13.3 %all-to-all-start.2 = ((f32[16,1,128]{2,1,0:T(1,128)}), f32[16,1,128]{2,1,0:T(1,128)S(1)}, u32[]{:S(2)}, u32[]{:S(2)}) async-start(f32[16,1,128]{2,1,0:T(1,128)} %spread.1), calls=%async_computation.2 | async-start | bytes 16384 | tf_op jit(solution)/shard_map/all_to_all | solution.py:307

commit v10 on v9

--- a/solution.py
+++ b/solution.py
@@ -48,8 +48,9 @@
             copy.start()
     _, start = polar_start()
     for l in range(LEVELS):
-        for copy in copies[l]:
-            copy.wait()
+        if l % 2 == 0:
+            for copy in (*copies[l], *copies[l + 1]):
+                copy.wait()
         source_t[pl.ds(l, CELLS, stride=LEVELS), :] = source[l].T
         courant_t[pl.ds(l, CELLS, stride=LEVELS), :] = factor[l].T
         for side in range(2):

time: 62.2 us -> 62.1 us (level)
  no operation moved by 1% of the time
where the time goes in v10:
time: 62.1 us; the launch traced here: 61.8 us
  blocking collectives  29.5 us (48%)
  starting transfers between devices  16.6 us (27%)
  waiting for transfers between devices  8.8 us (14%)
  Pallas kernels  6.18 us (10%)
  between operations  0.69 us (1%)
    all_to_all x2, blocking collectives, exchange(): return lax.all_to_all(blocks, 'ring', 0, 0, tiled=True).reshape(rows.shape)  29.5 us
    ppermute x1, starting transfers between devices, body(): far = lax.ppermute(got, every, across(True))  9.49 us
    all_to_all x1, starting transfers between devices, body(): sums = lax.all_to_all(spread(back, lats), 'lat', 0, 0, tiled=True)  6.49 us
    all_to_all x1, waiting for transfers between devices, body(): sums = lax.all_to_all(spread(back, lats), 'lat', 0, 0, tiled=True)  5.29 us
    ppermute x1, waiting for transfers between devices, body(): far = lax.ppermute(got, every, across(True))  3.5 us
    pallas_call x1, Pallas kernels, pack(): pl.pallas_call(pack_kernel, out_shape=(pltpu.VMEM((RING * SENT, 128), f32...  2.41 us
    pallas_call x1, Pallas kernels, finish(): pl.pallas_call(finish_kernel, out_shape=jax.ShapeDtypeStruct((LEVELS, ROW...  1.49 us
  transfers between devices with their start and end apart: 3, of which 2 were waited for; matrix products, arithmetic and copies ran while one was open for 0% of the time, Pallas kernels for 2%

profile of v10, /device:TPU:1, one launch (start us, length us, event | category | flops | bytes accessed | tf_op | source)
XLA Modules:
  0.0 61.8 jit_solution(9620110977498291543)
XLA Ops:
  0.6 2.4 %pack.1 = (f32[272,128]{1,0:T(8,128)S(1)}, f32[2048,128]{1,0:T(8,128)S(1)}, f32[2048,128]{1,0:T(8,128)S(1)}, f32[16,8,128]{2,1,0:T(8,128)S(1)}, s32[1,128]{1,0:T(1,128)S(1)}, /*index=5*/f32[1,128]{1,0:T(1,128)S(1)}) custom-call(f32[8,128,256]{2,1,0:T(8,128)} %tracer.1, f32[8,128,256]{2,1,0:T(8,128)} %courant.1, s32[1,128]{1,0:T(1,128)} %bitcast.13, ...), custom_call_target="tpu_custom_call" | custom-call | tf_op jit(solution)/shard_map/pack/pallas_call | solution.py:86
  3.0 18.6 %all_to_all.15 = f32[16,17,1,128]{3,2,1,0:T(1,128)S(1)} all-to-all(f32[16,17,1,128]{3,2,1,0:T(1,128)S(1)} %bitcast.12), channel_id=1, replica_groups=mesh['half'=2,'ring'=16,'lat'=16] {'ring'}, dimensions={0} | all-to-all | bytes 278528 | tf_op jit(solution)/shard_map/all_to_all | solution.py:286
  21.6 9.5 %collective-permute-start = (f32[272,128]{1,0:T(8,128)S(1)}, f32[272,128]{1,0:T(8,128)S(1)}, u32[]{:S(2)}, u32[]{:S(2)}) collective-permute-start(f32[272,128]{1,0:T(8,128)S(1)} %bitcast.8), channel_id=1, source_target_pairs={{0,256},{1,1},{2,2},{3,3},{4,4},{5,5},{6,6},{7,7},{8,8},{9,9},{10,... | collective-permute-start | bytes 417800 | tf_op jit(solution)/shard_map/ppermute | solution.py:304
  31.2 0.7 %collective-permute-start.1 = (f32[16,128]{1,0:T(8,128)S(1)}, f32[16,128]{1,0:T(8,128)S(1)}, u32[]{:S(2)}, u32[]{:S(2)}) collective-permute-start(f32[16,128]{1,0:T(8,128)S(1)} %slice.3), channel_id=1, source_target_pairs={{0,0},{1,257},{2,258},{3,259},{4,260},{5,261},{6,262},{7,263},{8,2... | collective-permute-start | bytes 24584 | tf_op jit(solution)/shard_map/ppermute | solution.py:305
  31.8 0.0 collective-permute-done.1.far_maps
  31.8 3.5 %collective-permute-done.far = f32[272,128]{1,0:T(8,128)S(1)} collective-permute-done((f32[272,128]{1,0:T(8,128)S(1)}, f32[272,128]{1,0:T(8,128)S(1)}, u32[]{:S(2)}, u32[]{:S(2)}) %collective-permute-start) | collective-permute-done | bytes 139296 | tf_op jit(solution)/shard_map/ppermute | solution.py:304
  35.3 1.0 %solve.1 = f32[144,128]{1,0:T(8,128)S(1)} custom-call(s32[1,128]{1,0:T(1,128)S(1)} %get-tuple-element.11.hops, f32[1,128]{1,0:T(1,128)S(1)} %get-tuple-element.12.area, f32[272,128]{1,0:T(8,128)S(1)} %bitcast.10, f32[272,128]{1,0:T(8,128)S(1)} %collective-permute-done.far, f32[16,128]{1,0:T(8,128)S(1)} %collective-permute-done.1.far_maps), custom_call_target="tpu_custom_call" | custom-call | tf_op jit(solution)/shard_map/solve/pallas_call | solution.py:195
  36.3 10.9 %all_to_all.16 = f32[16,9,1,128]{3,2,1,0:T(1,128)S(1)} all-to-all(f32[16,9,1,128]{3,2,1,0:T(1,128)S(1)} %bitcast.11), channel_id=1, replica_groups=mesh['half'=2,'ring'=16,'lat'=16] {'ring'}, dimensions={0} | all-to-all | bytes 147456 | tf_op jit(solution)/shard_map/all_to_all | solution.py:286
  47.2 0.7 %spread.1 = f32[16,1,128]{2,1,0:T(1,128)} custom-call(f32[144,128]{1,0:T(8,128)S(1)} %bitcast.6), custom_call_target="tpu_custom_call" | custom-call | tf_op jit(solution)/shard_map/spread/pallas_call | solution.py:212
  47.9 6.5 %all-to-all-start.2 = ((f32[16,1,128]{2,1,0:T(1,128)}), f32[16,1,128]{2,1,0:T(1,128)S(1)}, u32[]{:S(2)}, u32[]{:S(2)}) async-start(f32[16,1,128]{2,1,0:T(1,128)} %spread.1), calls=%async_computation.2 | async-start | bytes 16384 | tf_op jit(solution)/shard_map/all_to_all | solution.py:308
  54.4 1.5 %finish.1 = f32[8,128,256]{2,1,0:T(8,128)} custom-call(f32[2048,128]{1,0:T(8,128)S(1)} %get-tuple-element.8.source_t, f32[2048,128]{1,0:T(8,128)S(1)} %get-tuple-element.9.courant_t, f32[16,8,128]{2,1,0:T(8,128)S(1)} %get-tuple-element.10.entries, f32[144,128]{1,0:T(8,128)S(1)} %bitcast.7), custom_call_target="tpu_custom_call" | custom-call | tf_op jit(solution)/shard_map/finish/pallas_call | solution.py:270
  55.9 5.3 %all-to-all-done.2.sums = f32[16,1,128]{2,1,0:T(1,128)S(1)} async-done(((f32[16,1,128]{2,1,0:T(1,128)}), f32[16,1,128]{2,1,0:T(1,128)S(1)}, u32[]{:S(2)}, u32[]{:S(2)}) %all-to-all-start.2) | async-done | bytes 8224 | tf_op jit(solution)/shard_map/all_to_all | solution.py:308
  61.2 0.6 mean.1
  (1 shorter events, 0.0 us)
Async XLA Ops:
  21.6 13.7 %collective-permute-start = (f32[272,128]{1,0:T(8,128)S(1)}, f32[272,128]{1,0:T(8,128)S(1)}, u32[]{:S(2)}, u32[]{:S(2)}) collective-permute-start(f32[272,128]{1,0:T(8,128)S(1)} %bitcast.8), channel_id=1, source_target_pairs={{0,256},{1,1},{2,2},{3,3},{4,4},{5,5},{6,6},{7,7},{8,8},{9,9},{10,... | collective-permute-start | bytes 417800 | tf_op jit(solution)/shard_map/ppermute | solution.py:304
  31.2 0.7 %collective-permute-start.1 = (f32[16,128]{1,0:T(8,128)S(1)}, f32[16,128]{1,0:T(8,128)S(1)}, u32[]{:S(2)}, u32[]{:S(2)}) collective-permute-start(f32[16,128]{1,0:T(8,128)S(1)} %slice.3), channel_id=1, source_target_pairs={{0,0},{1,257},{2,258},{3,259},{4,260},{5,261},{6,262},{7,263},{8,2... | collective-permute-start | bytes 24584 | tf_op jit(solution)/shard_map/ppermute | solution.py:305
  47.9 13.3 %all-to-all-start.2 = ((f32[16,1,128]{2,1,0:T(1,128)}), f32[16,1,128]{2,1,0:T(1,128)S(1)}, u32[]{:S(2)}, u32[]{:S(2)}) async-start(f32[16,1,128]{2,1,0:T(1,128)} %spread.1), calls=%async_computation.2 | async-start | bytes 16384 | tf_op jit(solution)/shard_map/all_to_all | solution.py:308
